TPU v7x, 512 devices: a whole 4x8x8 slice. The times are simulated.
512 devices in a mesh: row: 16 (over y_lo, x, core), col: 8 (over z), seq: 4 (over y_hi).
Axes of the slice: x: 4, y: 8 (y_hi: 4, y_lo: 2; y = y_hi * 2 + y_lo), z: 8, core: 2. Of those that a mesh axis runs over, the one named last changes fastest.
Arguments:
- left_piece: bfloat16 [512, 32, 1024], P('seq', None, 'row'), may hold values from -6 to 6
- right_piece: bfloat16 [512, 32, 1024], P('seq', 'row', 'col'), may hold values from -6 to 6
- proj_weight: bfloat16 [1024, 128], replicated, may hold values from -4 to 4
- proj_bias: float32 [128], replicated, may hold values from -3 to 3
- pair_rep: bfloat16 [1024, 1024, 128], P(('row', 'seq'), 'col'), may hold values from -6 to 6
- norm_gain: float32 [128], replicated, may hold values from 0.5 to 1.5
- up_weight: bfloat16 [128, 512], replicated, may hold values from -0.5 to 0.5
- up_bias: float32 [512], replicated, may hold values from -3 to 3
- down_weight: bfloat16 [512, 128], replicated, may hold values from -0.25 to 0.25
- down_bias: float32 [128], replicated, may hold values from -3 to 3
Outputs:
- refined: bfloat16 [1024, 1024, 128], P(('row', 'seq'), 'col')
All inputs are finite; a program needn't handle non-finite values.
Results may differ from a plain program's by a relative error of at most 0.0085.
Values may be sent and summed in bfloat16 or wider, within the bound.
A program may use at most 64 MiB of HBM per device.

v0:
```python
import jax
import jax.numpy as jnp
from jax import lax
from jax.sharding import PartitionSpec as P

epsilon = 1e-05


def project_block(row_slab, right_all, proj_weight):
    seq_count, channels, row_count = row_slab.shape
    columns = right_all.shape[2]
    left_mat = row_slab.reshape(seq_count, channels * row_count)
    right_mat = right_all.reshape(seq_count, channels * columns)
    outer_prod = lax.dot_general(
        left_mat, right_mat, (((0,), (0,)), ((), ())), preferred_element_type=jnp.float32
    ).astype(jnp.bfloat16)
    outer_prod = outer_prod.reshape(channels, row_count, channels, columns).transpose(1, 3, 0, 2)
    outer_prod = outer_prod.reshape(row_count * columns, channels * channels)
    result = jnp.dot(outer_prod, proj_weight, preferred_element_type=jnp.float32)
    return result.reshape(row_count, columns, proj_weight.shape[1])


def project_rows(row_slab, right_all, proj_weight):
    seq_count, channels, row_count = row_slab.shape
    sub_rows = 8
    pieces = row_slab.reshape(seq_count, channels, row_count // sub_rows, sub_rows)
    pieces = jnp.moveaxis(pieces, 2, 0)
    result = lax.map(lambda portion: project_block(portion, right_all, proj_weight), pieces)
    return result.reshape(row_count, right_all.shape[2], proj_weight.shape[1])


def transition(middle, norm_gain, up_weight, up_bias, down_weight, down_bias):
    row_count, columns, channels = middle.shape
    values = middle.astype(jnp.float32).reshape(row_count * columns, channels)
    center = jnp.mean(values, axis=1, keepdims=True)
    spread = jnp.mean(jnp.square(values - center), axis=1, keepdims=True)
    normed = ((values - center) * lax.rsqrt(spread + epsilon) * norm_gain).astype(jnp.bfloat16)
    hidden = jnp.maximum(
        jnp.dot(normed, up_weight, preferred_element_type=jnp.float32) + up_bias, 0.0
    ).astype(jnp.bfloat16)
    result = values + jnp.dot(hidden, down_weight, preferred_element_type=jnp.float32) + down_bias
    return result.astype(jnp.bfloat16).reshape(row_count, columns, channels)


def gather_right(right_part):
    return lax.all_gather(right_part, "row", axis=1, tiled=True)


def move_cols(tile):
    return lax.all_to_all(tile, "col", split_axis=0, concat_axis=2, tiled=True)


def on_device(
    left_piece,
    right_piece,
    proj_weight,
    proj_bias,
    pair_rep,
    norm_gain,
    up_weight,
    up_bias,
    down_weight,
    down_bias,
):
    own_rows = pair_rep.shape[0]
    columns = pair_rep.shape[1]
    channels = pair_rep.shape[2]
    groups = lax.axis_size("seq")
    seq_index = lax.axis_index("seq")
    group_len = left_piece.shape[0]
    seq_total = group_len * groups
    left_all, right_seq = (
        lax.all_gather(left_piece, "seq", axis=0, tiled=True),
        lax.all_gather(right_piece, "seq", axis=0, tiled=True),
    )
    right_all = gather_right(right_seq)
    offset = seq_index * own_rows
    summed = jnp.zeros((own_rows, columns, channels), jnp.float32)
    for group_id in range(groups):
        left_group = left_all[group_id * group_len : (group_id + 1) * group_len]
        row_slab = lax.dynamic_slice_in_dim(left_group, offset, own_rows, 2)
        right_group = right_all[group_id * group_len : (group_id + 1) * group_len]
        summed = summed + project_rows(row_slab, right_group, proj_weight)
    update = (summed / seq_total + proj_bias).astype(jnp.bfloat16)
    col_count = lax.axis_size("col")
    rowseq_count = lax.axis_size(("row", "seq"))
    run_len = own_rows // col_count
    section_one = move_cols(update.reshape(col_count, run_len, columns, channels))
    section_two = lax.all_to_all(
        section_one.reshape(run_len, rowseq_count, own_rows, channels),
        ("row", "seq"),
        split_axis=1,
        concat_axis=0,
        tiled=True,
    )
    section_three = move_cols(
        section_two.reshape(col_count, rowseq_count // col_count, 1, run_len, own_rows, channels)
    )
    mirrored = section_three.reshape(columns, own_rows, channels).transpose(1, 0, 2)
    middle = (
        pair_rep.astype(jnp.float32)
        + 0.5 * (update.astype(jnp.float32) + mirrored.astype(jnp.float32))
    ).astype(jnp.bfloat16)
    return transition(middle, norm_gain, up_weight, up_bias, down_weight, down_bias)


def solution(mesh):
    in_specs = (
        P("seq", None, "row"),
        P("seq", "row", "col"),
        P(),
        P(),
        P(("row", "seq"), "col", None),
        P(),
        P(),
        P(),
        P(),
        P(),
    )
    out_specs = P(("row", "seq"), "col", None)
    return jax.shard_map(
        on_device, mesh=mesh, in_specs=in_specs, out_specs=out_specs, check_vma=False
    )
```

profile of v0, /device:TPU:1, one launch (start us, length us, event | category | flops | bytes accessed | tf_op | source)
XLA Modules:
  0.0 234.8 jit_solution(6227691487281684803)
XLA Ops:
  6.5 0.7 all-gather.3.cloned.1.call-update
  7.3 0.0 all-gather.5.cloned.1.call-start
  7.3 15.7 %all_gather.10 = bf16[512,2,128]{2,1,0:T(2,128)(2,1)S(1)} all-gather(bf16[128,2,128]{2,1,0:T(2,128)(2,1)} %param.19), channel_id=1, replica_groups=mesh['row'=16,'col'=8,'seq'=4] {'seq'}, dimensions={0}, use_global_device_ids=true | all-gather | bytes 327680 | tf_op jit(solution)/shard_map/all_gather | solution.py:74
  23.0 0.7 copy.100
  23.7 0.0 all-gather.5.cloned.1.call-update
  23.8 43.0 %all-gather.3.cloned.1.call-done = bf16[512,32,64]{0,2,1:T(8,128)(2,1)} async-done(((bf16[128,32,64]{0,2,1:T(8,128)(2,1)}), bf16[512,32,64]{0,2,1:T(8,128)(2,1)}) %all-gather.3.cloned.1.call-update) | async-done | bytes 2097168 | tf_op jit(solution)/shard_map/all_gather | solution.py:73
  66.7 1.8 fusion.68
  68.5 0.7 dynamic-slice_bitcast_fusion.2
  69.2 0.7 dynamic-slice_bitcast_fusion
  69.9 46.1 %all-gather.5.cloned.1.call-done = bf16[512,32,128]{2,0,1:T(8,128)(2,1)} async-done(((bf16[512,2,128]{2,0,1:T(8,128)(2,1)}), bf16[512,32,128]{2,0,1:T(8,128)(2,1)}) %all-gather.5.cloned.1.call-update) | async-done | bytes 4194320 | tf_op jit(solution)/shard_map/all_gather | solution.py:46
  116.0 2.8 %fusion.67 = (bf16[128,32,128]{2,0,1:T(8,128)(2,1)S(1)}, bf16[128,32,128]{2,0,1:T(8,128)(2,1)S(1)}, bf16[128,32,128]{2,0,1:T(8,128)(2,1)S(1)}, bf16[128,32,128]{2,0,1:T(8,128)(2,1)S(1)}) fusion(bf16[512,32,128]{2,0,1:T(8,128)(2,1)} %all-gather.5.cloned.1.call-done), kind=kLoop, calls=%fused_computation.71 | loop fusion | bytes 8388608 | tf_op jit(solution)/shard_map/slice | solution.py:82
  118.8 0.7 copy.104
  119.5 0.7 copy.108
  120.2 0.7 copy.106
  120.9 1.7 copy.102
  122.6 1.1 broadcast.42.clone.2
  123.7 7.8 %while.40 = (s32[]{:T(128)}, f32[2,8,128,128]{3,2,1,0:T(8,128)}, bf16[2,128,32,8]{1,3,0,2:T(8,128)(2,1)}, bf16[128,32,128]{2,1,0:T(8,128)(2,1)}, bf16[1024,128]{1,0:T(8,128)(2,1)}, /*index=5*/s32[]{:T(128)}) while((s32[]{:T(128)}, f32[2,8,128,128]{3,2,1,0:T(8,128)}, bf16[2,128,32,8]{1,3,0,2:T(8,128)(2,1)}, bf16[128,32,128]{2,1,0:T(8,128)(2,1)}, ...), condition=%wide.region_1.2_spmd, body=%wide.region_0.1_spmd.sunk | while | flops 537919488 | bytes 15532201 | solution.py:28
  123.7 2.1 convolution_convert_fusion.8
  125.8 0.8 fusion.96
  126.6 1.0 copy-done.2
  127.6 2.1 convolution_convert_fusion.8
  129.7 0.8 fusion.96
  130.5 1.0 copy-done.2
  131.5 1.1 broadcast.42.clone.1
  132.5 6.9 %while.42 = (s32[]{:T(128)}, f32[2,8,128,128]{3,2,1,0:T(8,128)}, bf16[2,128,32,8]{1,3,0,2:T(8,128)(2,1)}, bf16[128,32,128]{2,1,0:T(8,128)(2,1)S(1)}, bf16[1024,128]{1,0:T(8,128)(2,1)}, /*index=5*/s32[]{:T(128)}) while((s32[]{:T(128)}, f32[2,8,128,128]{3,2,1,0:T(8,128)}, bf16[2,128,32,8]{1,3,0,2:T(8,128)(2,1)}, ...), condition=%wide.region_5.6_spmd, body=%wide.region_4.5_spmd.sunk | while | flops 537919488 | bytes 15532201 | solution.py:28
  132.5 1.7 convolution_convert_fusion.10
  134.2 0.8 fusion.106
  135.0 1.0 copy-done.5
  136.0 1.7 convolution_convert_fusion.10
  137.7 0.8 fusion.106
  138.5 1.0 copy-done.5
  139.5 0.1 broadcast.42.clone
  139.6 3.5 %while.43 = (s32[]{:T(128)}, f32[2,8,128,128]{3,2,1,0:T(8,128)S(1)}, bf16[2,128,32,8]{1,3,0,2:T(8,128)(2,1)S(1)}, bf16[128,32,128]{2,1,0:T(8,128)(2,1)S(1)}, bf16[1024,128]{1,0:T(8,128)(2,1)}, /*index=5*/s32[]{:T(128)}) while((s32[]{:T(128)}, f32[2,8,128,128]{3,2,1,0:T(8,128)S(1)}, bf16[2,128,32,8]{1,3,0,2:T(8,128)(2,1)S(1)}, ...), condition=%wide.region_7.8_spmd, body=%wide.region_6.7_spmd.sunk | while | flops 537919488 | bytes 7143537 | solution.py:28
  139.6 0.7 convolution_convert_fusion.11
  140.3 0.2 copy-done.12
  140.5 0.8 fusion.111
  141.3 0.8 convolution_convert_fusion.11
  142.1 0.2 copy-done.12
  142.3 0.8 fusion.111
  143.1 0.1 broadcast.42.clone.3
  143.2 0.9 copy-done.6
  144.1 3.6 %while.41 = (s32[]{:T(128)}, f32[2,8,128,128]{3,2,1,0:T(8,128)S(1)}, bf16[2,128,32,8]{1,3,0,2:T(8,128)(2,1)S(1)}, bf16[128,32,128]{2,1,0:T(8,128)(2,1)S(1)}, bf16[1024,128]{1,0:T(8,128)(2,1)}, /*index=5*/s32[]{:T(128)}) while((s32[]{:T(128)}, f32[2,8,128,128]{3,2,1,0:T(8,128)S(1)}, bf16[2,128,32,8]{1,3,0,2:T(8,128)(2,1)S(1)}, ...), condition=%wide.region_3.4_spmd, body=%wide.region_2.3_spmd.sunk | while | flops 537919488 | bytes 7143537 | solution.py:28
  144.1 0.7 convolution_convert_fusion.9
  144.8 0.3 copy-done.13
  145.1 0.8 fusion.101
  145.9 0.8 convolution_convert_fusion.9
  146.7 0.2 copy-done.13
  146.9 0.8 fusion.101
  147.7 1.8 add_multiply_fusion
  149.6 0.1 add_convert_fusion
  149.7 24.2 %all_to_all.39 = bf16[8,2,128,128]{3,2,1,0:T(8,128)(2,1)S(1)} all-to-all(bf16[8,2,128,128]{3,2,1,0:T(8,128)(2,1)S(1)} %add_convert_fusion), channel_id=1, replica_groups=mesh['row'=16,'col'=8,'seq'=4] {'col'}, dimensions={0} | all-to-all | bytes 1048576 | tf_op jit(solution)/shard_map/all_to_all | solution.py:50
  174.0 28.1 %all_to_all.40 = bf16[2,64,16,128]{3,2,0,1:T(8,128)(2,1)S(1)} all-to-all(bf16[2,64,16,128]{3,2,0,1:T(8,128)(2,1)S(1)} %copy.111), channel_id=1, replica_groups=mesh['row'=16,'col'=8,'seq'=4] {'row','seq'}, dimensions={1} | all-to-all | bytes 1048576 | tf_op jit(solution)/shard_map/all_to_all | solution.py:89
  202.1 20.6 %all_to_all.41 = bf16[8,8,1,2,16,128]{5,4,3,1,2,0:T(8,128)(2,1)S(1)} all-to-all(bf16[8,8,1,2,16,128]{5,4,3,1,2,0:T(8,128)(2,1)S(1)} %bitcast.205), channel_id=1, replica_groups=mesh['row'=16,'col'=8,'seq'=4] {'col'}, dimensions={0} | all-to-all | bytes 1048576 | tf_op jit(solution)/shard_map/all_to_all | solution.py:50
  222.7 0.1 bitcast_convert_fusion
  222.8 1.0 fusion.60
  223.8 0.3 convert_reduce_fusion
  224.2 0.1 copy.114
  224.3 0.1 copy.115
  224.4 0.1 copy.116
  224.5 0.6 multiply_reduce_fusion
  225.2 0.1 copy.117
  225.2 0.0 copy-done.9
  225.2 0.6 fusion.63
  225.9 2.0 fusion.57
  (45 shorter events, 0.2 us)
Async XLA Ops:
  6.5 219.3 %copy-start = (bf16[512,128]{1,0:T(8,128)(2,1)S(1)}, bf16[512,128]{1,0:T(8,128)(2,1)}, u32[]{:S(2)}) copy-start(bf16[512,128]{1,0:T(8,128)(2,1)} %param.26) | copy-start | bytes 393220
  6.5 60.2 %all-gather.3.cloned.1.call-start = ((), (), s32[]{:S(2)}) async-start(), calls=%async_computation.3 | async-start | bytes 2621440 | tf_op jit(solution)/shard_map/all_gather | solution.py:73
  7.3 108.8 %all-gather.5.cloned.1.call-start = ((), (), s32[]{:S(2)}) async-start(), calls=%async_computation.4 | async-start | bytes 4456448 | tf_op jit(solution)/shard_map/all_gather | solution.py:46
  123.7 2.1 copy-start.1
  123.7 2.1 copy-start.10
  126.6 1.0 copy-start.2
  127.6 2.1 copy-start.1
  127.6 2.1 copy-start.10
  130.5 1.0 copy-start.2
  132.5 1.7 copy-start.4
  132.5 1.7 copy-start.11
  135.0 1.0 copy-start.5
  136.0 1.7 copy-start.4
  136.0 1.7 copy-start.11
  138.5 1.0 copy-start.5
  139.6 1.0 copy-start.12
  141.3 1.0 copy-start.12
  143.1 1.0 copy-start.6
  144.1 3.6 %copy-start.3 = (f32[2,8,128,128]{3,2,1,0:T(8,128)S(1)}, f32[2,8,128,128]{3,2,1,0:T(8,128)}, u32[]{:S(2)}) copy-start(f32[2,8,128,128]{3,2,1,0:T(8,128)} %get-tuple-element.113) | copy-start | bytes 3145732
  144.1 1.0 copy-start.13
  145.9 1.0 copy-start.13
  147.7 1.9 copy-start.8
  174.0 48.8 %copy-start.7 = (bf16[16,128,128]{2,1,0:T(8,128)(2,1)S(1)}, bf16[16,128,128]{2,1,0:T(8,128)(2,1)}, u32[]{:S(2)}) copy-start(bf16[16,128,128]{2,1,0:T(8,128)(2,1)} %param.22) | copy-start | bytes 1572868
  223.8 1.4 copy-start.9
  224.2 1.7 copy-start.14
  224.2 1.7 copy-start.15
  224.2 1.7 copy-start.16
Sparse Core Ops, SparseCore 0:
  9.4 57.2 all-gather.2
  68.9 47.1 all-gather.4
where the time goes:
time: 235 us
  waiting for transfers between devices  89.8 us (38%)
  blocking collectives  88.6 us (38%)
  local copies, waits for them, and re-layouts  18.9 us (8%)
  matrix products  18.8 us (8%)
  between operations  13.7 us (6%)
  other arithmetic  4.69 us (2%)
    all_gather x1, waiting for transfers between devices, gather_right(): return lax.all_gather(right_part, 'row', axis=1, tiled=True)  46.1 us
    all_to_all x2, blocking collectives, move_cols(): return lax.all_to_all(tile, 'col', split_axis=0, concat_axis=2, tiled=True)  44.8 us
    all_gather x1, waiting for transfers between devices, on_device(): lax.all_gather(left_piece, 'seq', axis=0, tiled=True)  43 us
    all_to_all x1, blocking collectives, on_device(): lax.all_to_all(section_one.reshape(run_len, rowseq_count, own_rows, chann...  28.1 us
    all_gather x1, blocking collectives, on_device(): lax.all_gather(right_piece, 'seq', axis=0, tiled=True)  15.7 us
    dot_general x8, matrix products, project_block(): lax.dot_general(left_mat, right_mat, (((0,), (0,)), ((), ())), preferred_...  10.5 us
    dot_general x8, matrix products, project_block(): jnp.dot(outer_prod, proj_weight, preferred_element_type=jnp.float32)  6.24 us
    while x32, local copies, waits for them, and re-layouts  4.73 us
  transfers between devices with their start and end apart: 2, of which 2 were waited for; matrix products, arithmetic and copies ran while one was open for 2% of the time, Pallas kernels for 0%

commit v1 on v0

v1 whole, which is shorter than its diff:
```python
import jax
import jax.numpy as jnp
from jax import lax
from jax.experimental import pallas as pl
from jax.experimental.pallas import tpu as pltpu
from jax.sharding import PartitionSpec as P

epsilon = 1e-05
MESH = pl.DeviceIdType.MESH
NX, NY, NZ = 4, 8, 8


def gather_kernel(
    r_loc, r_own, l_piece, l_own, r_all, l_all, own,
    s_a, g_a, s_b, g_b, s_c, g_c, s_z, g_z, s_self,
    s_rx, g_rx, s_rr, g_rr, s_rl, g_rl, s_rp, g_rp,
    s_lx, g_lx, s_lr, g_lr, s_ll, g_ll, s_lp, g_lp,
):
    r = lax.axis_index("row")
    z = lax.axis_index("col")
    q = lax.axis_index("seq")
    c = lax.rem(r, 2)
    p = lax.div(r, 2)
    x = lax.rem(p, NX)
    y = 2 * q + lax.div(p, NX)

    def dev(xx, yy, cc, zz):
        return {
            "row": (lax.rem(yy, 2) * NX + xx) * 2 + cc,
            "col": zz,
            "seq": lax.div(yy, 2),
        }

    def at(pp, cc, qq, zz):
        return {"row": pp * 2 + cc, "col": zz, "seq": qq}

    partner = dev(x, y, 1 - c, z)
    up = dev(x, lax.rem(y + 1, NY), c, z)
    down = dev(x, lax.rem(y + NY - 1, NY), c, z)
    x_plus = [dev(lax.rem(x + k, NX), y, c, z) for k in range(NX)]
    diagonal = p == z

    def send(src, dst, ssem, rsem, device):
        return pltpu.make_async_remote_copy(
            src_ref=src, dst_ref=dst, send_sem=ssem, recv_sem=rsem,
            device_id=device, device_id_type=MESH,
        )

    def rblk(k, dy):
        xx = lax.rem(x + NX - k, NX)
        yy = lax.rem(y + NY - dy, NY)
        return r_all.at[(lax.rem(yy, 2) * NX + xx) * 2 + c, lax.div(yy, 2)]

    def lblk(k, dy):
        xx = lax.rem(x + NX - k, NX)
        yy = lax.rem(y + NY - dy, NY)
        return l_all.at[(lax.rem(yy, 2) * NX + xx) * 2 + c, lax.div(yy, 2)]

    barrier = pltpu.get_barrier_semaphore()

    def greet(device):
        pl.semaphore_signal(barrier, inc=1, device_id=device, device_id_type=MESH)

    greet(partner)
    greet(up)
    greet(down)
    for k in range(1, NX):
        greet(x_plus[k])

    @pl.loop(1, NZ)
    def _(k):
        greet(at(p, c, q, lax.rem(z + k, NZ)))

    @pl.loop(1, 4)
    def _(k):
        greet(at(p, c, lax.rem(q + k, 4), z))

    @pl.loop(0, 8)
    def _(k):
        cc, qq = lax.div(k, 4), lax.rem(k, 4)

        @pl.when(jnp.logical_not(diagonal & (cc == c) & (qq == q)))
        def _():
            greet(at(z, cc, qq, p))

    pl.semaphore_wait(barrier, 24 - diagonal.astype(jnp.int32))

    def r_up(t, k):
        return send(rblk(k, t), rblk(k, t), s_rr.at[t, k], g_rr.at[t, k], up)

    def r_down(t, k):
        dy = lax.rem(NY - t, NY)
        return send(rblk(k, dy), rblk(k, dy), s_rl.at[t, k], g_rl.at[t, k], down)

    def r_pair(k, dy):
        return send(rblk(k, dy), rblk(k, dy), s_rp.at[dy, k], g_rp.at[dy, k], partner)

    def l_up(t):
        return send(lblk(0, t), lblk(0, t), s_lr.at[t], g_lr.at[t], up)

    def l_down(t):
        dy = lax.rem(NY - t, NY)
        return send(lblk(0, dy), lblk(0, dy), s_ll.at[t], g_ll.at[t], down)

    def l_x(k, dy):
        return send(lblk(0, dy), lblk(0, dy), s_lx.at[dy, k], g_lx.at[dy, k], x_plus[k])

    def l_pair(k, dy):
        return send(lblk(k, dy), lblk(k, dy), s_lp.at[dy, k], g_lp.at[dy, k], partner)

    def got(ref, sem):
        send(ref, ref, s_self.at[0], sem, partner).wait_recv()

    mine_r = rblk(0, 0)

    def a_copy(cc):
        return send(
            l_piece.at[cc], l_all.at[2 * z + cc, q, c], s_a.at[cc], g_a.at[c],
            at(z, cc, q, p),
        )

    def b_copy(k):
        cc, qq = lax.div(k, 4), lax.rem(k, 4)
        lanes = pl.ds(pl.multiple_of(q * 128, 128), 128)
        rows = pl.ds(pl.multiple_of(c * 32, 32), 32)
        return send(
            r_own.at[k], own.at[p, 1, rows, lanes], s_b.at[k], g_b.at[c * 4 + q],
            at(z, cc, qq, p),
        )

    def own_left():
        lanes = pl.ds(pl.multiple_of(q * 128, 128), 128)
        return own.at[z, 0, :, lanes]

    def c_copy(k):
        qq = lax.rem(q + k, 4)
        return send(
            l_own.at[qq], own_left(), s_c.at[k], g_c.at[k], at(p, c, qq, z)
        )

    first_x = [
        send(r_loc, mine_r, s_rx.at[k], g_rx.at[k], x_plus[k]) for k in range(1, NX)
    ]
    first_up = send(r_loc, mine_r, s_rr.at[0, 0], g_rr.at[0, 0], up)
    first_down = send(r_loc, mine_r, s_rl.at[0, 0], g_rl.at[0, 0], down)
    first_pair = send(r_loc, mine_r, s_rp.at[0, 0], g_rp.at[0, 0], partner)

    for cc in range(2):
        to_self = diagonal & (c == cc)

        @pl.when(jnp.logical_not(to_self))
        def _():
            a_copy(cc).start()

        @pl.when(to_self)
        def _():
            pltpu.make_async_copy(
                l_piece.at[cc], l_all.at[2 * z + cc, q, c], g_a.at[c]
            ).start()

    first_up.start()
    first_down.start()
    for k in range(1, NX):
        first_x[k - 1].start()

    @pl.loop(0, 8)
    def _(k):
        cc, qq = lax.div(k, 4), lax.rem(k, 4)
        to_self = diagonal & (cc == c) & (qq == q)

        @pl.when(jnp.logical_not(to_self))
        def _():
            b_copy(k).start()

        @pl.when(to_self)
        def _():
            lanes = pl.ds(pl.multiple_of(q * 128, 128), 128)
            rows = pl.ds(pl.multiple_of(c * 32, 32), 32)
            pltpu.make_async_copy(
                r_own.at[k], own.at[p, 1, rows, lanes], g_b.at[c * 4 + q]
            ).start()

    @pl.loop(1, 4)
    def _(k):
        c_copy(k).start()

    pltpu.make_async_copy(l_own.at[q], own_left(), g_c.at[0]).start()
    first_pair.start()
    self_copy = pltpu.make_async_copy(r_loc, mine_r, s_self.at[1])
    self_copy.start()

    for cc in range(2):
        got(l_all.at[r, q, cc], g_a.at[cc])
    l_up(0).start()
    l_down(0).start()
    for k in range(1, NX):
        l_x(k, 0).start()
    l_pair(0, 0).start()

    @pl.loop(1, NX)
    def _(k):
        got(rblk(k, 0), g_rx.at[k])
        r_up(0, k).start()
        r_down(0, k).start()
        r_pair(k, 0).start()

    @pl.loop(0, 8)
    def _(k):
        cc, qq = lax.div(k, 4), lax.rem(k, 4)
        lanes = pl.ds(pl.multiple_of(qq * 128, 128), 128)
        rows = pl.ds(pl.multiple_of(cc * 32, 32), 32)
        got(own.at[z, 1, rows, lanes], g_b.at[k])

    @pl.loop(0, 4)
    def _(k):
        qq = lax.rem(q + 4 - k, 4)
        lanes = pl.ds(pl.multiple_of(qq * 128, 128), 128)
        got(own.at[z, 0, :, lanes], g_c.at[k])

    def z_copy(k):
        return send(
            own.at[z], own.at[z], s_z.at[k], g_z.at[k], at(p, c, q, lax.rem(z + k, NZ))
        )

    @pl.loop(1, NZ)
    def _(k):
        z_copy(k).start()

    def x_arrivals(dy):
        for k in range(1, NX):
            got(lblk(k, dy), g_lx.at[dy, k])
            l_pair(k, dy).start()

    @pl.loop(1, 5)
    def _(t):
        got(lblk(0, t), g_lr.at[t - 1])

        @pl.when(t < 4)
        def _():
            l_up(t).start()

        for k in range(1, NX):
            l_x(k, t).start()
        l_pair(0, t).start()

        @pl.when(t < 4)
        def _():
            got(lblk(0, NY - t), g_ll.at[t - 1])

            @pl.when(t < 3)
            def _():
                l_down(t).start()

            for k in range(1, NX):
                l_x(k, NY - t).start()
            l_pair(0, NY - t).start()

        @pl.loop(0, NX)
        def _(k):
            got(rblk(k, t), g_rr.at[t - 1, k])

            @pl.when(t < 4)
            def _():
                r_up(t, k).start()

            r_pair(k, t).start()

            @pl.when(t < 4)
            def _():
                got(rblk(k, NY - t), g_rl.at[t - 1, k])

                @pl.when(t < 3)
                def _():
                    r_down(t, k).start()

                r_pair(k, NY - t).start()

        x_arrivals(t - 1)

        @pl.when(t > 1)
        def _():
            x_arrivals(NY + 1 - t)

    x_arrivals(4)

    @pl.loop(1, NZ)
    def _(k):
        zz = lax.rem(z + NZ - k, NZ)
        got(own.at[zz], g_z.at[k])

    def other(ref, k, dy):
        xx = lax.rem(x + NX - k, NX)
        yy = lax.rem(y + NY - dy, NY)
        return ref.at[(lax.rem(yy, 2) * NX + xx) * 2 + 1 - c, lax.div(yy, 2)]

    @pl.loop(0, NY)
    def _(dy):
        for k in range(NX):
            got(other(r_all, k, dy), g_rp.at[dy, k])
            got(other(l_all, k, dy), g_lp.at[dy, k])
            r_pair(k, dy).wait_send()
            l_pair(k, dy).wait_send()
            if k > 0:
                l_x(k, dy).wait_send()

    self_copy.wait()
    for cc in range(2):

        @pl.when(jnp.logical_not(diagonal & (c == cc)))
        def _():
            a_copy(cc).wait_send()

    @pl.loop(0, 8)
    def _(k):
        cc, qq = lax.div(k, 4), lax.rem(k, 4)

        @pl.when(jnp.logical_not(diagonal & (cc == c) & (qq == q)))
        def _():
            b_copy(k).wait_send()

    for k in range(1, 4):
        c_copy(k).wait_send()
        first_x[k - 1].wait_send()

    @pl.loop(1, NZ)
    def _(k):
        z_copy(k).wait_send()

    @pl.loop(0, 4)
    def _(t):
        l_up(t).wait_send()
        for k in range(NX):
            r_up(t, k).wait_send()

    @pl.loop(0, 3)
    def _(t):
        l_down(t).wait_send()
        for k in range(NX):
            r_down(t, k).wait_send()


def gather(r_loc, r_own, l_piece, l_own):
    dma = pltpu.SemaphoreType.DMA
    sems = []
    for shape in (
        (2,), (8,), (4,), (8,), None, (4,), (4, 4), (3, 4), (8, 4),
        (8, 4), (4,), (3,), (8, 4),
    ):
        if shape is None:
            sems.append(dma((2,)))
        else:
            sems.extend([dma(shape), dma(shape)])
    any_spec = pl.BlockSpec(memory_space=pl.ANY)
    return pl.pallas_call(
        gather_kernel,
        out_shape=(
            jax.ShapeDtypeStruct((16, 4, 128, 256), jnp.bfloat16),
            jax.ShapeDtypeStruct((16, 4, 2, 128, 128), jnp.bfloat16),
            jax.ShapeDtypeStruct((8, 2, 64, 512), jnp.bfloat16),
        ),
        in_specs=[any_spec] * 4,
        out_specs=(any_spec,) * 3,
        scratch_shapes=sems,
        compiler_params=pltpu.CompilerParams(collective_id=0, has_side_effects=True),
        name="gather_pieces",
    )(r_loc, r_own, l_piece, l_own)


def compute_kernel(
    r_ref, l_ref, own_ref, wd_ref, wm_ref, pair_ref, bias_ref, gain_ref,
    up_ref, upb_ref, down_ref, downb_ref, out_ref, lhs_l, lhs_r, wide, acc,
):
    step = pl.program_id(0)

    @pl.when(step == 0)
    def _():
        lhs_l[...] = own_ref[:, 0].reshape(512, 512)
        for k in range(4):
            lanes = slice(k * 128, (k + 1) * 128)
            wide[k] = own_ref[:, 1, :, lanes].reshape(512, 128).astype(jnp.float32)
            for i in range(16):
                lhs_r[i * 32 : (i + 1) * 32, lanes] = wide[
                    k, pl.ds(i, 32, stride=16), :
                ].astype(jnp.bfloat16)

    def project(lhs, pieces, weight):
        tiles = []
        for piece in pieces:
            full = jnp.dot(lhs, piece, preferred_element_type=jnp.float32)
            full = full.astype(jnp.bfloat16)
            tiles.append(full[:, :128])
            tiles.append(full[:, 128:])
        stacked = jnp.concatenate(
            [
                jnp.concatenate([tile[i * 32 : (i + 1) * 32] for tile in tiles], axis=0)
                for i in range(16)
            ],
            axis=1,
        )
        return jnp.dot(weight, stacked, preferred_element_type=jnp.float32)

    right = [r_ref[k].reshape(512, 256) for k in range(4)]
    left = []
    for k in range(4):
        low = l_ref[k, :, 0].reshape(512, 128)
        high = l_ref[k, :, 1].reshape(512, 128)
        left.append(
            jnp.concatenate(
                [low[:, :64], high[:, :64], low[:, 64:], high[:, 64:]], axis=1
            )
        )
    total = project(lhs_l[...], right, wd_ref[...]) + project(lhs_r[...], left, wm_ref[...])

    @pl.when(step == 0)
    def _():
        acc[...] = total

    @pl.when(step > 0)
    def _():
        acc[...] += total

    @pl.when(step == 3)
    def _():
        for i in range(16):
            both = acc[:, i * 128 : (i + 1) * 128].T
            middle = (
                pair_ref[i].astype(jnp.float32)
                + both * (0.5 / 512.0)
                + bias_ref[...]
            )
            values = middle.astype(jnp.bfloat16).astype(jnp.float32)
            center = jnp.mean(values, axis=1, keepdims=True)
            spread = jnp.mean(jnp.square(values - center), axis=1, keepdims=True)
            normed = (values - center) * lax.rsqrt(spread + epsilon) * gain_ref[...]
            hidden = jnp.dot(
                normed.astype(jnp.bfloat16), up_ref[...], preferred_element_type=jnp.float32
            )
            hidden = jnp.maximum(hidden + upb_ref[...], 0.0).astype(jnp.bfloat16)
            result = jnp.dot(hidden, down_ref[...], preferred_element_type=jnp.float32)
            out_ref[i] = (values + result + downb_ref[...]).astype(jnp.bfloat16)


def compute(r_all, l_all, own, wd, wm, pair, bias, gain, up, upb, down, downb):
    def whole(shape):
        return pl.BlockSpec(shape, lambda g: (0,) * len(shape))

    return pl.pallas_call(
        compute_kernel,
        out_shape=jax.ShapeDtypeStruct((16, 128, 128), jnp.bfloat16),
        grid=(4,),
        in_specs=[
            pl.BlockSpec((4, 4, 128, 256), lambda g: (g, 0, 0, 0)),
            pl.BlockSpec((4, 4, 2, 128, 128), lambda g: (g, 0, 0, 0, 0)),
            whole((8, 2, 64, 512)),
            pl.BlockSpec((128, 256), lambda g: (0, g)),
            pl.BlockSpec((128, 256), lambda g: (0, g)),
            whole((16, 128, 128)),
            whole((1, 128)),
            whole((1, 128)),
            whole((128, 512)),
            whole((1, 512)),
            whole((512, 128)),
            whole((1, 128)),
        ],
        out_specs=whole((16, 128, 128)),
        scratch_shapes=[
            pltpu.VMEM((512, 512), jnp.bfloat16),
            pltpu.VMEM((512, 512), jnp.bfloat16),
            pltpu.VMEM((4, 512, 128), jnp.float32),
            pltpu.VMEM((128, 2048), jnp.float32),
        ],
        compiler_params=pltpu.CompilerParams(vmem_limit_bytes=56 << 20),
        name="project_and_refine",
    )(r_all, l_all, own, wd, wm, pair, bias, gain, up, upb, down, downb)


def on_device(
    left_piece, right_piece, proj_weight, proj_bias, pair_rep, norm_gain,
    up_weight, up_bias, down_weight, down_bias,
):
    z = lax.axis_index("col")
    r_loc = right_piece.reshape(128, 256)
    r_own = right_piece.reshape(128, 2, 8, 16).transpose(2, 1, 3, 0).reshape(8, 32, 128)
    l_piece = lax.dynamic_slice_in_dim(left_piece, z * 4, 4, 1)
    l_piece = l_piece.reshape(128, 2, 128).transpose(1, 0, 2)
    l_own = lax.dynamic_slice_in_dim(left_piece.reshape(128, 32, 4, 16), z * 2, 2, 3)
    l_own = l_own.transpose(2, 3, 1, 0).reshape(4, 64, 128)
    weight = proj_weight.reshape(32, 32, 128)
    wd = weight.transpose(2, 1, 0).reshape(128, 1024)
    wm = proj_weight.T
    r_all, l_all, own = gather(r_loc, r_own, l_piece, l_own)
    return compute(
        r_all, l_all, own, wd, wm, pair_rep, proj_bias.reshape(1, 128),
        norm_gain.reshape(1, 128), up_weight, up_bias.reshape(1, 512), down_weight,
        down_bias.reshape(1, 128),
    )


def solution(mesh):
    in_specs = (
        P("seq", None, "row"), P("seq", "row", "col"), P(), P(),
        P(("row", "seq"), "col", None), P(), P(), P(), P(), P(),
    )
    out_specs = P(("row", "seq"), "col", None)
    return jax.shard_map(
        on_device, mesh=mesh, in_specs=in_specs, out_specs=out_specs, check_vma=False
    )
```

time: 235 us -> 85.2 us (0.36)
  waiting for transfers between devices: 89.8 us -> 0 us
  blocking collectives: 88.6 us -> 0 us
  Pallas kernels: 0 us -> 75.6 us
  matrix products: 18.8 us -> 0 us
  between operations: 13.7 us -> 0.02 us
  local copies, waits for them, and re-layouts: 18.9 us -> 9.24 us
  other arithmetic: 4.69 us -> 0 us
    all_gather x2 -> x0, waiting for transfers between devices: 89.1 us -> none  [the longest x1 46.1 us: gather_right(): return lax.all_gather(right_part, 'row', axis=1, tiled=True)]
    pallas_call x0 -> x2, Pallas kernels: none -> 75.6 us  [the longest x1 60.9 us: gather(): pl.pallas_call(gather_kernel, out_shape=(jax.ShapeDtypeStruct((16, 4, 128...]
    all_to_all x3 -> x0, blocking collectives: 72.9 us -> none  [the longest x2 44.8 us: move_cols(): return lax.all_to_all(tile, 'col', split_axis=0, concat_axis=2, tiled=True)]
    dot_general x17 -> x0, matrix products: 18.8 us -> none  [the longest x8 10.5 us: project_block(): lax.dot_general(left_mat, right_mat, (((0,), (0,)), ((), ())), preferred_...]
    all_gather x1 -> x0, blocking collectives: 15.7 us -> none  [on_device(): lax.all_gather(right_piece, 'seq', axis=0, tiled=True)]
    while x36 -> x0, local copies, waits for them, and re-layouts: 8.47 us -> none
    unnamed x18 -> x6, local copies, waits for them, and re-layouts: 0.97 us -> 5.9 us
    slice x2 -> x0, local copies, waits for them, and re-layouts: 4.54 us -> none  [the longest x1 2.76 us: on_device(): right_group = right_all[group_id * group_len:(group_id + 1) * group_len]]
  transfers between devices with their start and end apart: 2 -> 0, of which waited for: 2 -> 0; matrix products, arithmetic and copies ran while one was open for 2% -> 0% of each run, Pallas kernels for 0% -> 0%
where the time goes in v1:
time: 85.2 us; the launch traced here: 84.9 us
  Pallas kernels  75.6 us (89%)
  local copies, waits for them, and re-layouts  9.24 us (11%)
    pallas_call x1, Pallas kernels, gather(): pl.pallas_call(gather_kernel, out_shape=(jax.ShapeDtypeStruct((16, 4, 128...  60.9 us
    pallas_call x1, Pallas kernels, compute(): pl.pallas_call(compute_kernel, out_shape=jax.ShapeDtypeStruct((16, 128, 1...  14.7 us
    unnamed x6, local copies, waits for them, and re-layouts  5.9 us

profile of v1, /device:TPU:1, one launch (start us, length us, event | category | flops | bytes accessed | tf_op | source)
XLA Modules:
  0.0 84.9 jit_solution(2382276649545543890)
XLA Ops:
  0.0 0.0 copy-start
  0.0 1.0 %copy-done = bf16[128,32,64]{0,2,1:T(8,128)(2,1)S(1)} copy-done((bf16[128,32,64]{0,2,1:T(8,128)(2,1)S(1)}, bf16[128,32,64]{0,2,1:T(8,128)(2,1)}, u32[]{:S(2)}) %copy-start) | copy-done | bytes 524312
  1.0 0.1 constant_dynamic-slice_fusion
  1.1 0.6 copy.28
  1.8 0.7 copy.23
  2.5 1.5 %copy.31 = bf16[16,8,2,128]{3,1,2,0:T(8,128)(2,1)} copy(bf16[16,8,2,128]{3,2,1,0:T(2,128)(2,1)} %bitcast.27) | data formatting | bytes 131072
  4.0 1.0 %copy.21 = bf16[128,2,128]{0,2,1:T(8,128)(2,1)S(1)} copy(bf16[128,2,128]{2,1,0:T(2,128)(2,1)} %param.11) | data formatting | bytes 131072 | tf_op args[1]
  4.9 0.6 copy.22
  5.6 1.1 %copy.25 = bf16[128,32,32]{0,2,1:T(8,128)(2,1)S(1)} copy(bf16[128,32,32]{0,1,2:T(8,128)(2,1)} %bitcast.25) | data formatting | bytes 524288 | tf_op jit(solution)/shard_map/transpose | solution.py:489
  6.6 0.9 %copy.27.wd_ref = bf16[128,1024]{1,0:T(8,128)(2,1)} copy(bf16[128,1024]{0,1:T(8,128)(2,1)S(1)} %bitcast.26) | data formatting | bytes 524288 | tf_op jit(solution)/shard_map/reshape | solution.py:489
  7.5 1.8 %copy.26 = bf16[1024,128]{0,1:T(8,128)(2,1)} copy(bf16[1024,128]{1,0:T(8,128)(2,1)} %param.12) | data formatting | bytes 524288 | tf_op args[2]
  9.3 60.9 %gather_pieces.1 = (bf16[16,4,128,256]{3,2,1,0:T(8,128)(2,1)}, bf16[16,4,2,128,128]{4,3,2,1,0:T(8,128)(2,1)}, bf16[8,2,64,512]{3,2,1,0:T(8,128)(2,1)}) custom-call(bf16[128,256]{1,0:T(8,128)(2,1)} %bitcast.32, bf16[8,32,128]{2,1,0:T(8,128)(2,1)} %bitcast.33, bf16[2,128,128]{2,1,0:T(8,128)(2,1)} %bitcast.31, bf16[4,64,128]{2,1,0:T(8,128)(2,1)} %bitcast.30), custom_call_target="tpu_custom_call" | custom-call | tf_op jit(solution)/shard_map/gather_pieces/pallas_call | solution.py:354
  70.1 14.7 %project_and_refine.1 = bf16[16,128,128]{2,1,0:T(8,128)(2,1)} custom-call(bf16[16,4,128,256]{3,2,1,0:T(8,128)(2,1)} %get-tuple-element.8.r_ref, bf16[16,4,2,128,128]{4,3,2,1,0:T(8,128)(2,1)} %get-tuple-element.9.l_ref, bf16[8,2,64,512]{3,2,1,0:T(8,128)(2,1)} %get-tuple-element.10.own_ref, bf16[128,1024]{1,0:T(8,128)(2,1)} %copy.27.wd_ref, ...), custom_call_target="tpu_custom_call" | custom-call | tf_op jit(solution)/shard_map/project_and_refine/pallas_call | solution.py:447
  (1 shorter events, 0.0 us)
Async XLA Ops:
  0.0 1.0 %copy-start = (bf16[128,32,64]{0,2,1:T(8,128)(2,1)S(1)}, bf16[128,32,64]{0,2,1:T(8,128)(2,1)}, u32[]{:S(2)}) copy-start(bf16[128,32,64]{0,2,1:T(8,128)(2,1)} %param.10) | copy-start | bytes 1572868

commit v2 on v0

v2 whole, which is shorter than its diff:
```python
import jax
import jax.numpy as jnp
from jax import lax
from jax.experimental import pallas as pl
from jax.experimental.pallas import tpu as pltpu
from jax.sharding import PartitionSpec as P

epsilon = 1e-05
MESH = pl.DeviceIdType.MESH
NX, NY, NZ = 4, 8, 8

SEMS = {
    "a": (2,), "b": (8,), "c": (4,), "z": (8,), "rx": (4,), "ru": (4, 4), "rd": (4, 4),
    "rp": (8, 4), "lx": (8, 4), "lu": (4,), "ld": (4,), "lp": (8, 4), "own": (8,),
}


def fused_kernel(
    l_src, r_src, w_src, pair_src, up_src, down_src, bias_ref, gain_ref, upb_ref,
    downb_ref, out_ref, r_all, l_all, own, r_own, lhs_l, lhs_r, wide, w_in, w_wide, wd,
    wm, pair, up_w, down_w, acc, *sems,
):
    names = list(SEMS)
    ssem = dict(zip(names, sems[: len(names)]))
    gsem = dict(zip(names, sems[len(names) :]))
    r = lax.axis_index("row")
    z = lax.axis_index("col")
    q = lax.axis_index("seq")
    c = lax.rem(r, 2)
    p = lax.div(r, 2)
    x = lax.rem(p, NX)
    ylo = lax.div(p, NX)
    y = 2 * q + ylo

    def dev(xx, yy, cc, zz):
        return {
            "row": (lax.rem(yy, 2) * NX + xx) * 2 + cc,
            "col": zz,
            "seq": lax.div(yy, 2),
        }

    def at(pp, cc, qq, zz):
        return {"row": pp * 2 + cc, "col": zz, "seq": qq}

    partner = dev(x, y, 1 - c, z)
    up = dev(x, lax.rem(y + 1, NY), c, z)
    down = dev(x, lax.rem(y + NY - 1, NY), c, z)
    east = dev(lax.rem(x + 1, NX), y, c, z)
    west = dev(lax.rem(x + NX - 1, NX), y, c, z)
    diagonal = p == z

    def send(src, dst, name, index, device, landing=None):
        landing = index if landing is None else landing
        return pltpu.make_async_remote_copy(
            src_ref=src, dst_ref=dst, send_sem=ssem[name].at[index],
            recv_sem=gsem[name].at[landing], device_id=device, device_id_type=MESH,
        )

    def got(ref, name, index):
        pltpu.make_async_remote_copy(
            src_ref=ref, dst_ref=ref, send_sem=ssem["own"].at[0],
            recv_sem=gsem[name].at[index], device_id=partner, device_id_type=MESH,
        ).wait_recv()

    def block(ref, k, dy, cc):
        xx = lax.rem(x + NX - k, NX)
        yy = lax.rem(y + NY - dy, NY)
        return ref.at[(lax.rem(yy, 2) * NX + xx) * 2 + cc, lax.div(yy, 2)]

    def rblk(k, dy):
        return block(r_all, k, dy, c)

    def lblk(k, dy):
        return block(l_all, k, dy, c)

    def rhalf(k, dy, side):
        return rblk(k, dy).at[pl.ds(side * 64, 64)]

    def lhalf(k, dy, side):
        return lblk(k, dy).at[side]

    def lanes_of(qq):
        return pl.ds(pl.multiple_of(qq * 128, 128), 128)

    barrier = pltpu.get_barrier_semaphore()

    def greet(device):
        pl.semaphore_signal(barrier, inc=1, device_id=device, device_id_type=MESH)

    for neighbour in (partner, up, down, east, west):
        greet(neighbour)

    @pl.loop(1, NZ)
    def _(k):
        greet(at(p, c, q, lax.rem(z + k, NZ)))

    @pl.loop(1, 4)
    def _(k):
        greet(at(p, c, lax.rem(q + k, 4), z))

    @pl.loop(0, 8)
    def _(k):
        cc, qq = lax.div(k, 4), lax.rem(k, 4)

        @pl.when(jnp.logical_not(diagonal & (cc == c) & (qq == q)))
        def _():
            greet(at(z, cc, qq, p))

    local = [
        pltpu.make_async_copy(src, dst, gsem["own"].at[i])
        for i, (src, dst) in enumerate(
            ((w_src, w_in), (pair_src, pair), (up_src, up_w), (down_src, down_w))
        )
    ]
    for copy in local:
        copy.start()

    mine = r_all.at[r, q]
    for e in range(2):
        plane = r_src[:, e, :]
        mine[:, e * 128 : (e + 1) * 128] = plane
        turned = plane.T
        for k in range(8):
            r_own[k, e] = turned[k * 16 : (k + 1) * 16]

    pl.semaphore_wait(barrier, 22 + 1 - diagonal.astype(jnp.int32))

    def a_copy(cc):
        return send(
            l_src.at[pl.ds(4 * z + 2 * cc, 2)], l_all.at[2 * z + cc, q, c], "a", cc,
            at(z, cc, q, p), c,
        )

    def b_copy(k):
        cc, qq = lax.div(k, 4), lax.rem(k, 4)
        return send(
            r_own.at[k], own.at[p, 1, pl.ds(2 * c, 2), :, lanes_of(q)], "b", k,
            at(z, cc, qq, p), c * 4 + q,
        )

    def c_source(qq):
        return l_src.at[pl.ds(4 * z, 4), pl.ds(pl.multiple_of(qq * 16, 16), 16)]

    def c_copy(k):
        qq = lax.rem(q + k, 4)
        return send(
            c_source(qq), own.at[z, 0, :, :, lanes_of(q)], "c", k, at(p, c, qq, z)
        )

    def z_copy(k):
        return send(own.at[z], own.at[z], "z", k, at(p, c, q, lax.rem(z + k, NZ)))

    def r_x(k):
        return send(mine, mine, "rx", k, east if k == 1 else west)

    def r_x_half(k):
        part = rhalf(k, 0, 0 if k == 1 else 1)
        return send(part, part, "rx", 2 if k == 1 else 0, east if k == 1 else west)

    def l_x(k, dy):
        return send(lblk(0, dy), lblk(0, dy), "lx", (dy, k), east if k == 1 else west)

    def l_x_half(k, dy):
        part = lhalf(k, dy, 0 if k == 1 else 1)
        slot = 2 if k == 1 else 0
        return send(part, part, "lx", (dy, slot), east if k == 1 else west)

    def r_up(t, k):
        ref = rblk(k, t) if t < 3 else rhalf(k, 3, 0)
        return send(ref, ref, "ru", (t, k), up)

    def r_down(t, k):
        ref = rblk(k, -t % NY) if t < 3 else rhalf(k, 5, 1)
        return send(ref, ref, "rd", (t, k), down)

    def l_up(t):
        ref = lblk(0, t) if t < 3 else lhalf(0, 3, 0)
        return send(ref, ref, "lu", t, up)

    def l_down(t):
        ref = lblk(0, -t % NY) if t < 3 else lhalf(0, 5, 1)
        return send(ref, ref, "ld", t, down)

    def r_pair(k, dy):
        return send(rblk(k, dy), rblk(k, dy), "rp", (dy, k), partner)

    def l_pair(k, dy):
        return send(lblk(k, dy), lblk(k, dy), "lp", (dy, k), partner)

    def is_self(cc, qq):
        return diagonal & (cc == c) & (qq == q)

    for cc in range(2):

        @pl.when(jnp.logical_not(is_self(cc, q)))
        def _():
            a_copy(cc).start()

        @pl.when(is_self(cc, q))
        def _():
            pltpu.make_async_copy(
                l_src.at[pl.ds(4 * z + 2 * cc, 2)], l_all.at[2 * z + cc, q, c],
                gsem["a"].at[c],
            ).start()

    r_x(1).start()
    r_x(3).start()
    r_up(0, 0).start()
    r_down(0, 0).start()

    @pl.loop(0, 8)
    def _(k):
        cc, qq = lax.div(k, 4), lax.rem(k, 4)

        @pl.when(jnp.logical_not(is_self(cc, qq)))
        def _():
            b_copy(k).start()

        @pl.when(is_self(cc, qq))
        def _():
            pltpu.make_async_copy(
                r_own.at[k], own.at[p, 1, pl.ds(2 * c, 2), :, lanes_of(q)],
                gsem["b"].at[c * 4 + q],
            ).start()

    @pl.loop(1, 4)
    def _(k):
        c_copy(k).start()

    pltpu.make_async_copy(
        c_source(q), own.at[z, 0, :, :, lanes_of(q)], gsem["c"].at[0]
    ).start()
    r_pair(0, 0).start()

    def l_arrive(dy):
        l_x(1, dy).start()
        l_x(3, dy).start()
        l_pair(0, dy).start()

    def l_step(t):
        if t < 4:
            got(lblk(0, t), "lu", t - 1)
            l_up(t).start()
            l_arrive(t)
            got(lblk(0, NY - t), "ld", t - 1)
            l_down(t).start()
            l_arrive(NY - t)
        else:
            got(lhalf(0, 4, 0), "lu", 3)
            got(lhalf(0, 4, 1), "ld", 3)
            l_arrive(4)

    def dys(t):
        return (t,) if t in (0, 4) else (t, NY - t)

    def l_sides(t):
        for dy in dys(t):
            for k in (1, 3):
                got(lblk(k, dy), "lx", (dy, k))
                l_x_half(k, dy).start()
                l_pair(k, dy).start()

    def l_far(t):
        for dy in dys(t):
            got(lhalf(2, dy, 0), "lx", (dy, 2))
            got(lhalf(2, dy, 1), "lx", (dy, 0))
            l_pair(2, dy).start()

    def r_step(t, k):
        if t < 4:
            got(rblk(k, t), "ru", (t - 1, k))
            r_up(t, k).start()
            r_pair(k, t).start()
            got(rblk(k, NY - t), "rd", (t - 1, k))
            r_down(t, k).start()
            r_pair(k, NY - t).start()
        else:
            got(rhalf(k, 4, 0), "ru", (3, k))
            got(rhalf(k, 4, 1), "rd", (3, k))
            r_pair(k, 4).start()

    def r_sides():
        for k in (1, 3):
            got(rblk(k, 0), "rx", k)
            r_x_half(k).start()
            r_up(0, k).start()
            r_down(0, k).start()
            r_pair(k, 0).start()

    def r_far():
        got(rhalf(2, 0, 0), "rx", 2)
        got(rhalf(2, 0, 1), "rx", 0)
        r_up(0, 2).start()
        r_down(0, 2).start()
        r_pair(2, 0).start()

    def project(group, lhs, pieces, weight):
        tiles = []
        for full in pieces(lhs):
            full = full.astype(jnp.bfloat16)
            tiles.append(full[:, :128])
            tiles.append(full[:, 128:])
        stacked = jnp.concatenate(
            [
                jnp.concatenate([tile[i * 32 : (i + 1) * 32] for tile in tiles], axis=0)
                for i in range(16)
            ],
            axis=1,
        )
        acc[...] += jnp.dot(weight[group], stacked, preferred_element_type=jnp.float32)

    def direct(yy, cc):
        def pieces(lhs):
            for k in range(NX):
                rhs = r_all[yy * 8 + 2 * k + cc].reshape(512, 256)
                yield jnp.dot(lhs, rhs, preferred_element_type=jnp.float32)

        project(yy * 2 + cc, lhs_l[...], pieces, wd)

    def mirror(yy, cc):
        def pieces(lhs):
            for k in range(NX):
                row = yy * 8 + 2 * k + cc
                rhs = jnp.concatenate(
                    [
                        jnp.concatenate(
                            [
                                l_all[row, qq, side, ch]
                                for ch in range(2)
                                for side in range(2)
                            ],
                            axis=0,
                        )
                        for qq in range(4)
                    ],
                    axis=1,
                )
                yield lax.dot_general(
                    lhs, rhs, (((1,), (1,)), ((), ())), preferred_element_type=jnp.float32
                )

        project(yy * 2 + cc, lhs_r[...], pieces, wm)

    def from_partner(ref, name, parity):
        for dy in range(parity, NY, 2):
            for k in range(NX):
                got(block(ref, k, dy, 1 - c), name, (dy, k))

    def prepare_weights():
        for copy in local:
            copy.wait()
        acc[...] = jnp.zeros_like(acc)
        w_wide[...] = w_in[...].astype(jnp.float32)
        for group in range(4):
            rows = [(group // 2) * 8 + 2 * k + group % 2 for k in range(NX)]
            order = [2 * row + e for row in rows for e in range(2)]
            wd[group] = (
                jnp.concatenate([w_wide[pl.ds(e, 32, stride=32), :] for e in order], axis=0)
                .T.astype(jnp.bfloat16)
            )
            wm[group] = (
                jnp.concatenate([w_wide[e * 32 : (e + 1) * 32, :] for e in order], axis=0)
                .T.astype(jnp.bfloat16)
            )

    def prepare_own():
        for side, lhs in ((0, lhs_l), (1, lhs_r)):
            for k in range(4):
                lanes = slice(k * 128, (k + 1) * 128)
                wide[k] = own[:, side, :, :, lanes].reshape(512, 128).astype(jnp.float32)
                for i in range(16):
                    lhs[i * 32 : (i + 1) * 32, lanes] = wide[
                        k, pl.ds(i, 32, stride=16), :
                    ].astype(jnp.bfloat16)

    for cc in range(2):
        got(l_all.at[r, q, cc], "a", cc)
    l_up(0).start()
    l_down(0).start()
    l_arrive(0)
    r_sides()

    @pl.loop(0, 8)
    def _(k):
        cc, qq = lax.div(k, 4), lax.rem(k, 4)
        got(own.at[z, 1, pl.ds(2 * cc, 2), :, lanes_of(qq)], "b", k)

    @pl.loop(0, 4)
    def _(k):
        qq = lax.rem(q + 4 - k, 4)
        got(own.at[z, 0, :, :, lanes_of(qq)], "c", k)

    @pl.loop(1, NZ)
    def _(k):
        z_copy(k).start()

    r_far()
    l_step(1)
    l_sides(0)
    r_step(1, 0)
    prepare_weights()
    for k in (1, 3):
        r_step(1, k)
    l_step(2)
    l_sides(1)
    l_far(0)
    r_step(1, 2)
    r_step(2, 0)
    l_step(3)
    l_sides(2)
    l_far(1)
    for k in (1, 3):
        r_step(2, k)
    l_step(4)
    l_sides(3)
    l_far(2)
    r_step(2, 2)
    r_step(3, 0)

    @pl.loop(1, NZ)
    def _(k):
        zz = lax.rem(z + NZ - k, NZ)
        got(own.at[zz], "z", k)

    prepare_own()
    l_sides(4)
    l_far(3)
    mirror(1 - ylo, c)
    for k in (1, 3, 2):
        r_step(3, k)
    l_far(4)
    from_partner(l_all, "lp", 1)
    mirror(1 - ylo, 1 - c)
    r_step(4, 0)
    mirror(ylo, c)
    for k in (1, 3, 2):
        r_step(4, k)
    from_partner(l_all, "lp", 0)
    mirror(ylo, 1 - c)
    from_partner(r_all, "rp", 1)
    direct(1 - ylo, c)
    direct(1 - ylo, 1 - c)
    direct(ylo, c)
    from_partner(r_all, "rp", 0)
    direct(ylo, 1 - c)

    for i in range(16):
        both = acc[:, i * 128 : (i + 1) * 128].T
        middle = pair[i].astype(jnp.float32) + both * (0.5 / 512.0) + bias_ref[...]
        values = middle.astype(jnp.bfloat16).astype(jnp.float32)
        center = jnp.mean(values, axis=1, keepdims=True)
        spread = jnp.mean(jnp.square(values - center), axis=1, keepdims=True)
        normed = (values - center) * lax.rsqrt(spread + epsilon) * gain_ref[...]
        hidden = jnp.dot(
            normed.astype(jnp.bfloat16), up_w[...], preferred_element_type=jnp.float32
        )
        hidden = jnp.maximum(hidden + upb_ref[...], 0.0).astype(jnp.bfloat16)
        result = jnp.dot(hidden, down_w[...], preferred_element_type=jnp.float32)
        out_ref[i] = (values + result + downb_ref[...]).astype(jnp.bfloat16)

    for cc in range(2):

        @pl.when(jnp.logical_not(is_self(cc, q)))
        def _():
            a_copy(cc).wait_send()

    @pl.loop(0, 8)
    def _(k):
        @pl.when(jnp.logical_not(is_self(lax.div(k, 4), lax.rem(k, 4))))
        def _():
            b_copy(k).wait_send()

    @pl.loop(1, 4)
    def _(k):
        c_copy(k).wait_send()

    @pl.loop(1, NZ)
    def _(k):
        z_copy(k).wait_send()

    for k in (1, 3):
        r_x(k).wait_send()
        r_x_half(k).wait_send()
    for t in range(4):
        l_up(t).wait_send()
        l_down(t).wait_send()
        for k in range(NX):
            r_up(t, k).wait_send()
            r_down(t, k).wait_send()

    @pl.loop(0, NY)
    def _(dy):
        for k in range(NX):
            r_pair(k, dy).wait_send()
            l_pair(k, dy).wait_send()
        for k in (1, 3):
            l_x(k, dy).wait_send()
            l_x_half(k, dy).wait_send()


def on_device(
    left_piece, right_piece, proj_weight, proj_bias, pair_rep, norm_gain,
    up_weight, up_bias, down_weight, down_bias,
):
    any_spec = pl.BlockSpec(memory_space=pl.ANY)
    near = pl.BlockSpec(memory_space=pltpu.VMEM)
    bf16, f32 = jnp.bfloat16, jnp.float32
    sems = [pltpu.SemaphoreType.DMA(shape) for shape in SEMS.values()]
    return pl.pallas_call(
        fused_kernel,
        out_shape=jax.ShapeDtypeStruct((16, 128, 128), bf16),
        in_specs=[any_spec, near] + [any_spec] * 4 + [near] * 4,
        out_specs=near,
        scratch_shapes=[
            pltpu.VMEM((16, 4, 128, 256), bf16),
            pltpu.VMEM((16, 4, 2, 2, 64, 128), bf16),
            pltpu.VMEM((8, 2, 4, 16, 512), bf16),
            pltpu.VMEM((8, 2, 16, 128), bf16),
            pltpu.VMEM((512, 512), bf16),
            pltpu.VMEM((512, 512), bf16),
            pltpu.VMEM((4, 512, 128), f32),
            pltpu.VMEM((1024, 128), bf16),
            pltpu.VMEM((1024, 128), f32),
            pltpu.VMEM((4, 128, 256), bf16),
            pltpu.VMEM((4, 128, 256), bf16),
            pltpu.VMEM((16, 128, 128), bf16),
            pltpu.VMEM((128, 512), bf16),
            pltpu.VMEM((512, 128), bf16),
            pltpu.VMEM((128, 2048), f32),
        ]
        + sems
        + sems,
        compiler_params=pltpu.CompilerParams(
            collective_id=0, has_side_effects=True, vmem_limit_bytes=56 << 20
        ),
        name="gather_and_refine",
    )(
        left_piece.transpose(1, 2, 0), right_piece, proj_weight, pair_rep, up_weight,
        down_weight, proj_bias.reshape(1, 128), norm_gain.reshape(1, 128),
        up_bias.reshape(1, 512), down_bias.reshape(1, 128),
    )


def solution(mesh):
    in_specs = (
        P("seq", None, "row"), P("seq", "row", "col"), P(), P(),
        P(("row", "seq"), "col", None), P(), P(), P(), P(), P(),
    )
    out_specs = P(("row", "seq"), "col", None)
    return jax.shard_map(
        on_device, mesh=mesh, in_specs=in_specs, out_specs=out_specs, check_vma=False
    )
```

time: 235 us -> 76.5 us (0.33)
  waiting for transfers between devices: 89.8 us -> 0 us
  blocking collectives: 88.6 us -> 0 us
  Pallas kernels: 0 us -> 74.3 us
  matrix products: 18.8 us -> 0 us
  local copies, waits for them, and re-layouts: 18.9 us -> 1.89 us
  between operations: 13.7 us -> 0.01 us
  other arithmetic: 4.69 us -> 0 us
    all_gather x2 -> x0, waiting for transfers between devices: 89.1 us -> none  [the longest x1 46.1 us: gather_right(): return lax.all_gather(right_part, 'row', axis=1, tiled=True)]
    pallas_call x0 -> x1, Pallas kernels: none -> 74.3 us  [on_device(): pl.pallas_call(fused_kernel, out_shape=jax.ShapeDtypeStruct((16, 128, 128...]
    all_to_all x3 -> x0, blocking collectives: 72.9 us -> none  [the longest x2 44.8 us: move_cols(): return lax.all_to_all(tile, 'col', split_axis=0, concat_axis=2, tiled=True)]
    dot_general x17 -> x0, matrix products: 18.8 us -> none  [the longest x8 10.5 us: project_block(): lax.dot_general(left_mat, right_mat, (((0,), (0,)), ((), ())), preferred_...]
    all_gather x1 -> x0, blocking collectives: 15.7 us -> none  [on_device(): lax.all_gather(right_piece, 'seq', axis=0, tiled=True)]
    while x36 -> x0, local copies, waits for them, and re-layouts: 8.47 us -> none
    slice x2 -> x0, local copies, waits for them, and re-layouts: 4.54 us -> none  [the longest x1 2.76 us: on_device(): right_group = right_all[group_id * group_len:(group_id + 1) * group_len]]
    another operation x4 -> x0, local copies, waits for them, and re-layouts: 2.35 us -> none
  transfers between devices with their start and end apart: 2 -> 0, of which waited for: 2 -> 0; matrix products, arithmetic and copies ran while one was open for 2% -> 0% of each run, Pallas kernels for 0% -> 0%
where the time goes in v2:
time: 76.5 us; the launch traced here: 76.2 us
  Pallas kernels  74.3 us (97%)
  local copies, waits for them, and re-layouts  1.89 us (2%)
    pallas_call x1, Pallas kernels, on_device(): pl.pallas_call(fused_kernel, out_shape=jax.ShapeDtypeStruct((16, 128, 128...  74.3 us
    unnamed x1, local copies, waits for them, and re-layouts  1.89 us

profile of v2, /device:TPU:1, one launch (start us, length us, event | category | flops | bytes accessed | tf_op | source)
XLA Modules:
  0.0 76.2 jit_solution(2829910153563280152)
XLA Ops:
  0.0 74.3 %gather_and_refine.1 = bf16[16,128,128]{2,1,0:T(8,128)(2,1)} custom-call(bf16[32,64,128]{2,1,0:T(8,128)(2,1)} %bitcast.5, bf16[128,2,128]{2,1,0:T(2,128)(2,1)} %r_src.1, bf16[1024,128]{1,0:T(8,128)(2,1)} %w_src.1, bf16[16,128,128]{2,1,0:T(8,128)(2,1)} %pair_src.1, bf16[128,512]{1,0:T(8,128)(2,1)} %up_src.1, bf16[512,128]{1,0:T(8,128)(2,1)} %down_src.1, ...), custom_call_target="tpu_custom_call" | custom-call | tf_op jit(solution)/shard_map/gather_and_refine/pallas_call | solution.py:509
  74.3 1.9 %copy.12 = bf16[16,128,128]{2,1,0:T(8,128)(2,1)} copy(bf16[16,128,128]{2,1,0:T(8,128)(2,1)} %gather_and_refine.1) | data formatting | bytes 1048576

commit v3 on v2

v3 whole, which is shorter than its diff:
```python
import jax
import jax.numpy as jnp
from jax import lax
from jax.experimental import pallas as pl
from jax.experimental.pallas import tpu as pltpu
from jax.sharding import PartitionSpec as P

epsilon = 1e-05
MESH = pl.DeviceIdType.MESH
NX, NY, NZ = 4, 8, 8

ARRIVALS = {
    "a": (1,), "b": (1,), "c": (1,), "z": (4, 2), "rx": (4,), "r": (4, 4), "rp": (2,),
    "lx": (5, 2), "l": (4,), "lp": (2,), "own": (4,),
}
DEPARTURES = ("a", "b", "c", "z", "r", "l", "near")
LEAVES_BY = {"rp": "r", "lx": "l", "lp": "l", "rx": "near", "l": "near"}


def fused_kernel(
    l_src, r_src, w_src, pair_src, up_src, down_src, bias_ref, gain_ref, upb_ref,
    downb_ref, out_ref, r_all, l_all, own, r_own, lhs_l, lhs_r, wide, w_in, w_wide, wd,
    wm, pair, up_w, down_w, acc, tokens, *sems,
):
    gsem = dict(zip(ARRIVALS, sems))
    ssem = dict(zip(DEPARTURES, (sems[-1].at[i] for i in range(len(DEPARTURES)))))
    r = lax.axis_index("row")
    z = lax.axis_index("col")
    q = lax.axis_index("seq")
    c = lax.rem(r, 2)
    p = lax.div(r, 2)
    x = lax.rem(p, NX)
    ylo = lax.div(p, NX)
    y = 2 * q + ylo

    def dev(xx, yy, cc, zz):
        return {
            "row": (lax.rem(yy, 2) * NX + xx) * 2 + cc,
            "col": zz,
            "seq": lax.div(yy, 2),
        }

    def at(pp, cc, qq, zz):
        return {"row": pp * 2 + cc, "col": zz, "seq": qq}

    partner = dev(x, y, 1 - c, z)
    up = dev(x, lax.rem(y + 1, NY), c, z)
    down = dev(x, lax.rem(y + NY - 1, NY), c, z)
    east = dev(lax.rem(x + 1, NX), y, c, z)
    west = dev(lax.rem(x + NX - 1, NX), y, c, z)
    diagonal = p == z

    def send(src, dst, name, landing, device):
        return pltpu.make_async_remote_copy(
            src_ref=src, dst_ref=dst, send_sem=ssem[LEAVES_BY.get(name, name)],
            recv_sem=gsem[name].at[landing], device_id=device, device_id_type=MESH,
        )

    def got(ref, name, index):
        pltpu.make_async_remote_copy(
            src_ref=ref, dst_ref=ref, send_sem=ssem["a"], recv_sem=gsem[name].at[index],
            device_id=partner, device_id_type=MESH,
        ).wait_recv()

    def left(ref, name):
        pltpu.make_async_remote_copy(
            src_ref=ref, dst_ref=ref, send_sem=ssem[name], recv_sem=gsem["a"].at[0],
            device_id=partner, device_id_type=MESH,
        ).wait_send()

    def block(ref, k, dy, cc):
        xx = lax.rem(x + NX - k, NX)
        yy = lax.rem(y + NY - dy, NY)
        return ref.at[(lax.rem(yy, 2) * NX + xx) * 2 + cc, lax.div(yy, 2)]

    def rblk(k, dy):
        return block(r_all, k, dy, c)

    def lblk(k, dy):
        return block(l_all, k, dy, c)

    def rhalf(k, dy, side):
        return rblk(k, dy).at[pl.ds(side * 64, 64)]

    def lhalf(k, dy, side):
        return lblk(k, dy).at[side]

    def lanes_of(qq):
        return pl.ds(pl.multiple_of(qq * 128, 128), 128)

    barrier = pltpu.get_barrier_semaphore()

    def greet(device):
        pl.semaphore_signal(barrier, inc=1, device_id=device, device_id_type=MESH)

    greet(partner)
    for k in range(1, NX):
        greet(dev(lax.rem(x + k, NX), y, c, z))

    @pl.loop(1, NY)
    def _(k):
        greet(dev(x, lax.rem(y + k, NY), c, z))
        greet(at(p, c, q, lax.rem(z + k, NZ)))

    for cc in range(2):

        @pl.when(jnp.logical_not(diagonal & (c == cc)))
        def _():
            greet(at(z, cc, q, z))

    local = [
        pltpu.make_async_copy(src, dst, gsem["own"].at[i])
        for i, (src, dst) in enumerate(
            ((w_src, w_in), (pair_src, pair), (up_src, up_w), (down_src, down_w))
        )
    ]
    for copy in local:
        copy.start()

    mine = r_all.at[r, q]
    for e in range(2):
        plane = r_src[:, e, :]
        mine[:, e * 128 : (e + 1) * 128] = plane
        turned = plane.T
        for k in range(8):
            r_own[k, e] = turned[k * 16 : (k + 1) * 16]

    def prepare_weights():
        for copy in local:
            copy.wait()
        acc[...] = jnp.zeros_like(acc)
        w_wide[...] = w_in[...].astype(jnp.float32)
        for group in range(4):
            rows = [(group // 2) * 8 + 2 * k + group % 2 for k in range(NX)]
            order = [2 * row + e for row in rows for e in range(2)]
            wd[group] = (
                jnp.concatenate([w_wide[pl.ds(e, 32, stride=32), :] for e in order], axis=0)
                .T.astype(jnp.bfloat16)
            )
            wm[group] = (
                jnp.concatenate([w_wide[e * 32 : (e + 1) * 32, :] for e in order], axis=0)
                .T.astype(jnp.bfloat16)
            )

    prepare_weights()
    pl.semaphore_wait(barrier, 18 + 15 * diagonal.astype(jnp.int32))

    def token(step, device):
        pl.semaphore_signal(tokens.at[step], inc=1, device_id=device, device_id_type=MESH)

    @pl.loop(1, NY)
    def _(k):
        token(0, dev(x, lax.rem(y + k, NY), c, z))

    def a_copy(row):
        return send(
            l_src.at[pl.ds(2 * row, 2)], l_all.at[row, q, c], "a", 0,
            {"row": row, "col": z, "seq": q},
        )

    def b_copy(k):
        cc, qq = lax.div(k, 4), lax.rem(k, 4)
        return send(
            r_own.at[k], own.at[p, 1, pl.ds(2 * c, 2), :, lanes_of(q)], "b", 0,
            at(z, cc, qq, p),
        )

    def c_source(qq):
        return l_src.at[pl.ds(4 * z, 4), pl.ds(pl.multiple_of(qq * 16, 16), 16)]

    def c_copy(k):
        qq = lax.rem(q + k, 4)
        return send(
            c_source(qq), own.at[z, 0, :, :, lanes_of(q)], "c", 0, at(p, c, qq, z)
        )

    def z_block(dz, side):
        return own.at[lax.rem(z + NZ - dz, NZ), side]

    def z_half(dz, side, part):
        return z_block(dz, side).at[pl.ds(2 * part, 2)]

    def z_up(t, side):
        ref = z_block(t, side) if t < 3 else z_half(3, side, 0)
        return send(ref, ref, "z", (t, side), at(p, c, q, lax.rem(z + 1, NZ)))

    def z_down(t, side):
        ref = z_block(-t % NZ, side) if t < 3 else z_half(5, side, 1)
        return send(ref, ref, "z", (t, side), at(p, c, q, lax.rem(z + NZ - 1, NZ)))

    def r_x(k):
        return send(mine, mine, "rx", k, east if k == 1 else west)

    def r_x_half(k):
        part = rhalf(k, 0, 0 if k == 1 else 1)
        return send(part, part, "rx", 2, east if k == 1 else west)

    def ring(dy):
        return min(dy, NY - dy)

    def l_x(k, dy):
        ref = lblk(0, dy)
        return send(ref, ref, "lx", (ring(dy), 0), east if k == 1 else west)

    def l_x_half(k, dy):
        part = lhalf(k, dy, 0 if k == 1 else 1)
        return send(part, part, "lx", (ring(dy), 1), east if k == 1 else west)

    def r_up(t, k):
        ref = rblk(k, t) if t < 3 else rhalf(k, 3, 0)
        return send(ref, ref, "r", (t, k), up)

    def r_down(t, k):
        ref = rblk(k, -t % NY) if t < 3 else rhalf(k, 5, 1)
        return send(ref, ref, "r", (t, k), down)

    def l_up(t):
        ref = lblk(0, t) if t < 3 else lhalf(0, 3, 0)
        return send(ref, ref, "l", t, up)

    def l_down(t):
        ref = lblk(0, -t % NY) if t < 3 else lhalf(0, 5, 1)
        return send(ref, ref, "l", t, down)

    def r_pair(k, dy):
        return send(rblk(k, dy), rblk(k, dy), "rp", dy % 2, partner)

    def l_pair(k, dy):
        return send(lblk(k, dy), lblk(k, dy), "lp", dy % 2, partner)

    def is_self(cc, qq):
        return diagonal & (cc == c) & (qq == q)

    r_up(0, 0).start()
    r_down(0, 0).start()
    r_x(1).start()
    r_x(3).start()

    @pl.when(diagonal)
    def _():
        pltpu.make_async_copy(
            l_src.at[pl.ds(2 * r, 2)], l_all.at[r, q, c], gsem["a"].at[0]
        ).start()

        @pl.loop(1, 16)
        def _(k):
            a_copy(lax.rem(r + k, 16)).start()

    @pl.loop(1, 4)
    def _(k):
        c_copy(k).start()

    pltpu.make_async_copy(
        c_source(q), own.at[z, 0, :, :, lanes_of(q)], gsem["c"].at[0]
    ).start()
    r_pair(0, 0).start()

    def l_arrive(dy):
        l_x(1, dy).start()
        l_x(3, dy).start()
        l_pair(0, dy).start()

    def l_step(t):
        got(l_all.at[0, pl.ds(0, 2 if t < 4 else 1)], "l", t - 1)
        if t < 4:
            l_up(t).start()
            l_down(t).start()
            l_arrive(t)
            l_arrive(NY - t)
        else:
            l_arrive(4)

    def dys(t):
        return (t,) if t in (0, 4) else (t, NY - t)

    def l_sides(t):
        got(l_all.at[0, pl.ds(0, 2 * len(dys(t)))], "lx", (t, 0))
        for dy in dys(t):
            for k in (1, 3):
                l_x_half(k, dy).start()
        for dy in dys(t):
            for k in (1, 3):
                l_pair(k, dy).start()

    def l_far(t):
        got(l_all.at[0, pl.ds(0, len(dys(t)))], "lx", (t, 1))
        for dy in dys(t):
            l_pair(2, dy).start()

    def r_step(t, k):
        got(r_all.at[0, pl.ds(0, 2 if t < 4 else 1)], "r", (t - 1, k))
        if t < 4:
            r_up(t, k).start()
            r_down(t, k).start()
            r_pair(k, t).start()
            r_pair(k, NY - t).start()
        else:
            r_pair(k, 4).start()

    def r_turn(k):
        got(rblk(k, 0), "rx", k)
        if k != 2:
            r_x_half(k).start()
        r_up(0, k).start()
        r_down(0, k).start()
        r_pair(k, 0).start()

    def project(group, lhs, pieces, weight):
        tiles = []
        for full in pieces(lhs):
            full = full.astype(jnp.bfloat16)
            tiles.append(full[:, :128])
            tiles.append(full[:, 128:])
        stacked = jnp.concatenate(
            [
                jnp.concatenate([tile[i * 32 : (i + 1) * 32] for tile in tiles], axis=0)
                for i in range(16)
            ],
            axis=1,
        )
        acc[...] += jnp.dot(weight[group], stacked, preferred_element_type=jnp.float32)

    def direct(yy, cc):
        def pieces(lhs):
            for k in range(NX):
                rhs = r_all[yy * 8 + 2 * k + cc].reshape(512, 256)
                yield jnp.dot(lhs, rhs, preferred_element_type=jnp.float32)

        project(yy * 2 + cc, lhs_l[...], pieces, wd)

    def mirror(yy, cc):
        def pieces(lhs):
            for k in range(NX):
                row = yy * 8 + 2 * k + cc
                rhs = jnp.concatenate(
                    [
                        jnp.concatenate(
                            [
                                l_all[row, qq, side, ch]
                                for ch in range(2)
                                for side in range(2)
                            ],
                            axis=0,
                        )
                        for qq in range(4)
                    ],
                    axis=1,
                )
                yield lax.dot_general(
                    lhs, rhs, (((1,), (1,)), ((), ())), preferred_element_type=jnp.float32
                )

        project(yy * 2 + cc, lhs_r[...], pieces, wm)

    def from_partner(ref, name, parity):
        got(ref.at[pl.ds(0, 4)], name, parity)

    def prepare_own(side, lhs):
        for k in range(4):
            lanes = slice(k * 128, (k + 1) * 128)
            wide[k] = own[:, side, :, :, lanes].reshape(512, 128).astype(jnp.float32)
            for i in range(16):
                lhs[i * 32 : (i + 1) * 32, lanes] = wide[
                    k, pl.ds(i, 32, stride=16), :
                ].astype(jnp.bfloat16)

    def own_left():
        got(own.at[z, 0], "c", 0)
        z_up(0, 0).start()
        z_down(0, 0).start()

    def own_right():
        got(own.at[z, 1], "b", 0)
        z_up(0, 1).start()
        z_down(0, 1).start()

    def z_step(t, side):
        got(own.at[0] if t < 4 else own.at[0, 0], "z", (t - 1, side))
        if t < 4:
            z_up(t, side).start()
            z_down(t, side).start()

    def own_send():
        @pl.loop(0, 8)
        def _(k):
            cc, qq = lax.div(k, 4), lax.rem(k, 4)

            @pl.when(jnp.logical_not(is_self(cc, qq)))
            def _():
                b_copy(k).start()

            @pl.when(is_self(cc, qq))
            def _():
                pltpu.make_async_copy(
                    r_own.at[k], own.at[p, 1, pl.ds(2 * c, 2), :, lanes_of(q)],
                    gsem["b"].at[0],
                ).start()

    r_turn(1)
    r_turn(3)
    pl.semaphore_wait(tokens.at[0], 7)

    @pl.loop(1, NZ)
    def _(k):
        token(1, at(p, c, q, lax.rem(z + k, NZ)))

    got(l_all.at[r, q], "a", 0)
    l_up(0).start()
    l_down(0).start()
    l_arrive(0)
    pl.semaphore_wait(tokens.at[1], 7)
    token(2, partner)
    r_step(1, 0)
    pl.semaphore_wait(tokens.at[2], 1)
    own_send()
    own_left()
    l_step(1)
    r_turn(2)
    r_step(1, 1)
    l_sides(0)
    z_step(1, 0)
    l_step(2)
    r_step(1, 3)
    r_step(1, 2)
    l_far(0)
    z_step(2, 0)
    l_sides(1)
    l_step(3)
    own_right()
    r_step(2, 0)
    r_step(2, 1)
    z_step(3, 0)
    l_far(1)
    l_step(4)
    r_step(2, 3)
    z_step(1, 1)
    l_sides(2)
    r_step(2, 2)
    z_step(4, 0)
    r_step(3, 0)
    z_step(2, 1)
    l_far(2)
    l_sides(3)
    r_step(3, 1)
    r_step(3, 3)
    z_step(3, 1)
    l_sides(4)
    l_far(3)
    r_step(3, 2)
    prepare_own(0, lhs_l)
    direct(1 - ylo, c)
    l_far(4)
    r_step(4, 0)
    from_partner(r_all, "rp", 1)
    direct(1 - ylo, 1 - c)
    r_step(4, 1)
    z_step(4, 1)
    prepare_own(1, lhs_r)
    from_partner(l_all, "lp", 1)
    mirror(1 - ylo, c)
    r_step(4, 3)
    mirror(1 - ylo, 1 - c)
    r_step(4, 2)
    from_partner(l_all, "lp", 0)
    mirror(ylo, c)
    mirror(ylo, 1 - c)
    direct(ylo, c)
    from_partner(r_all, "rp", 0)
    direct(ylo, 1 - c)

    for i in range(16):
        both = acc[:, i * 128 : (i + 1) * 128].T
        middle = pair[i].astype(jnp.float32) + both * (0.5 / 512.0) + bias_ref[...]
        values = middle.astype(jnp.bfloat16).astype(jnp.float32)
        center = jnp.mean(values, axis=1, keepdims=True)
        spread = jnp.mean(jnp.square(values - center), axis=1, keepdims=True)
        normed = (values - center) * lax.rsqrt(spread + epsilon) * gain_ref[...]
        hidden = jnp.dot(
            normed.astype(jnp.bfloat16), up_w[...], preferred_element_type=jnp.float32
        )
        hidden = jnp.maximum(hidden + upb_ref[...], 0.0).astype(jnp.bfloat16)
        result = jnp.dot(hidden, down_w[...], preferred_element_type=jnp.float32)
        out_ref[i] = (values + result + downb_ref[...]).astype(jnp.bfloat16)

    @pl.when(diagonal)
    def _():
        left(l_all.at[pl.ds(0, 15), 0, 0], "a")
        left(r_own.at[pl.ds(0, 7)], "b")

    @pl.when(jnp.logical_not(diagonal))
    def _():
        left(r_own, "b")

    left(own.at[pl.ds(0, 3), 0, :, :, pl.ds(0, 128)], "c")
    left(own.at[pl.ds(0, 7)], "z")
    left(r_all.at[pl.ds(0, 15)], "r")
    left(l_all.at[pl.ds(0, 14)], "l")
    left(l_all.at[pl.ds(0, 10), 0], "near")


def on_device(
    left_piece, right_piece, proj_weight, proj_bias, pair_rep, norm_gain,
    up_weight, up_bias, down_weight, down_bias,
):
    any_spec = pl.BlockSpec(memory_space=pl.ANY)
    near = pl.BlockSpec(memory_space=pltpu.VMEM)
    bf16, f32 = jnp.bfloat16, jnp.float32
    sems = [pltpu.SemaphoreType.DMA(shape) for shape in ARRIVALS.values()]
    return pl.pallas_call(
        fused_kernel,
        out_shape=jax.ShapeDtypeStruct((16, 128, 128), bf16),
        in_specs=[any_spec, near] + [any_spec] * 4 + [near] * 4,
        out_specs=near,
        scratch_shapes=[
            pltpu.VMEM((16, 4, 128, 256), bf16),
            pltpu.VMEM((16, 4, 2, 2, 64, 128), bf16),
            pltpu.VMEM((8, 2, 4, 16, 512), bf16),
            pltpu.VMEM((8, 2, 16, 128), bf16),
            pltpu.VMEM((512, 512), bf16),
            pltpu.VMEM((512, 512), bf16),
            pltpu.VMEM((4, 512, 128), f32),
            pltpu.VMEM((1024, 128), bf16),
            pltpu.VMEM((1024, 128), f32),
            pltpu.VMEM((4, 128, 256), bf16),
            pltpu.VMEM((4, 128, 256), bf16),
            pltpu.VMEM((16, 128, 128), bf16),
            pltpu.VMEM((128, 512), bf16),
            pltpu.VMEM((512, 128), bf16),
            pltpu.VMEM((128, 2048), f32),
            pltpu.SemaphoreType.REGULAR((3,)),
        ]
        + sems
        + [pltpu.SemaphoreType.DMA((len(DEPARTURES),))],
        compiler_params=pltpu.CompilerParams(
            collective_id=0, has_side_effects=True, vmem_limit_bytes=56 << 20
        ),
        name="gather_and_refine",
    )(
        left_piece.transpose(1, 2, 0), right_piece, proj_weight, pair_rep, up_weight,
        down_weight, proj_bias.reshape(1, 128), norm_gain.reshape(1, 128),
        up_bias.reshape(1, 512), down_bias.reshape(1, 128),
    )


def solution(mesh):
    in_specs = (
        P("seq", None, "row"), P("seq", "row", "col"), P(), P(),
        P(("row", "seq"), "col", None), P(), P(), P(), P(), P(),
    )
    out_specs = P(("row", "seq"), "col", None)
    return jax.shard_map(
        on_device, mesh=mesh, in_specs=in_specs, out_specs=out_specs, check_vma=False
    )
```

time: 76.5 us -> 68.8 us (0.90)
  Pallas kernels: 74.3 us -> 66.7 us
    pallas_call x1, Pallas kernels: 74.3 us -> 66.7 us  [on_device(): pl.pallas_call(fused_kernel, out_shape=jax.ShapeDtypeStruct((16, 128, 128...]
where the time goes in v3:
time: 68.8 us; the launch traced here: 68.6 us
  Pallas kernels  66.7 us (97%)
  local copies, waits for them, and re-layouts  1.89 us (3%)
    pallas_call x1, Pallas kernels, on_device(): pl.pallas_call(fused_kernel, out_shape=jax.ShapeDtypeStruct((16, 128, 128...  66.7 us
    unnamed x1, local copies, waits for them, and re-layouts  1.89 us

profile of v3, /device:TPU:1, one launch (start us, length us, event | category | flops | bytes accessed | tf_op | source)
XLA Modules:
  0.0 68.6 jit_solution(15979188131151857003)
XLA Ops:
  0.0 66.7 %gather_and_refine.1 = bf16[16,128,128]{2,1,0:T(8,128)(2,1)} custom-call(bf16[32,64,128]{2,1,0:T(8,128)(2,1)} %bitcast.5, bf16[128,2,128]{2,1,0:T(2,128)(2,1)} %r_src.1, bf16[1024,128]{1,0:T(8,128)(2,1)} %w_src.1, bf16[16,128,128]{2,1,0:T(8,128)(2,1)} %pair_src.1, bf16[128,512]{1,0:T(8,128)(2,1)} %up_src.1, bf16[512,128]{1,0:T(8,128)(2,1)} %down_src.1, ...), custom_call_target="tpu_custom_call" | custom-call | tf_op jit(solution)/shard_map/gather_and_refine/pallas_call | solution.py:509
  66.7 1.9 %copy.12 = bf16[16,128,128]{2,1,0:T(8,128)(2,1)} copy(bf16[16,128,128]{2,1,0:T(8,128)(2,1)} %gather_and_refine.1) | data formatting | bytes 1048576

commit v4 on v3

--- a/solution.py
+++ b/solution.py
@@ -8,18 +8,19 @@
 epsilon = 1e-05
 MESH = pl.DeviceIdType.MESH
 NX, NY, NZ = 4, 8, 8
+PARTS = 4
 
 ARRIVALS = {
     "a": (1,), "b": (1,), "c": (1,), "z": (4, 2), "rx": (4,), "r": (4, 4), "rp": (2,),
-    "lx": (5, 2), "l": (4,), "lp": (2,), "own": (4,),
+    "lx": (5, 2), "l": (4,), "lp": (2,), "own": (13,),
 }
 DEPARTURES = ("a", "b", "c", "z", "r", "l", "near")
 LEAVES_BY = {"rp": "r", "lx": "l", "lp": "l", "rx": "near", "l": "near"}
 
 
 def fused_kernel(
-    l_src, r_src, w_src, pair_src, up_src, down_src, bias_ref, gain_ref, upb_ref,
-    downb_ref, out_ref, r_all, l_all, own, r_own, lhs_l, lhs_r, wide, w_in, w_wide, wd,
+    l_src, r_src, w_src, pair_src, up_src, down_src, bias_src, gain_src, upb_src,
+    downb_src, out_ref, r_in, bias_ref, gain_ref, upb_ref, downb_ref, out_buf, r_all, l_all, own, r_own, lhs_l, lhs_r, wide, w_in, w_wide, wd,
     wm, pair, up_w, down_w, acc, tokens, *sems,
 ):
     gsem = dict(zip(ARRIVALS, sems))
@@ -93,6 +94,19 @@
     def greet(device):
         pl.semaphore_signal(barrier, inc=1, device_id=device, device_id_type=MESH)
 
+    local = [
+        pltpu.make_async_copy(src, dst, gsem["own"].at[i])
+        for i, (src, dst) in enumerate(
+            (
+                (w_src, w_in), (pair_src, pair), (up_src, up_w), (down_src, down_w),
+                (bias_src, bias_ref), (gain_src, gain_ref), (upb_src, upb_ref),
+                (downb_src, downb_ref),
+            )
+        )
+    ]
+    first = pltpu.make_async_copy(r_src, r_in, gsem["own"].at[8])
+    first.start()
+
     greet(partner)
     for k in range(1, NX):
         greet(dev(lax.rem(x + k, NX), y, c, z))
@@ -108,22 +122,19 @@
         def _():
             greet(at(z, cc, q, z))
 
-    local = [
-        pltpu.make_async_copy(src, dst, gsem["own"].at[i])
-        for i, (src, dst) in enumerate(
-            ((w_src, w_in), (pair_src, pair), (up_src, up_w), (down_src, down_w))
-        )
-    ]
     for copy in local:
         copy.start()
 
     mine = r_all.at[r, q]
+    first.wait()
     for e in range(2):
-        plane = r_src[:, e, :]
-        mine[:, e * 128 : (e + 1) * 128] = plane
-        turned = plane.T
-        for k in range(8):
-            r_own[k, e] = turned[k * 16 : (k + 1) * 16]
+        mine[:, e * 128 : (e + 1) * 128] = r_in[:, e, :]
+
+    def prepare_right():
+        for e in range(2):
+            turned = r_in[:, e, :].T
+            for k in range(8):
+                r_own[k, e] = turned[k * 16 : (k + 1) * 16]
 
     def prepare_weights():
         for copy in local:
@@ -142,7 +153,6 @@
                 .T.astype(jnp.bfloat16)
             )
 
-    prepare_weights()
     pl.semaphore_wait(barrier, 18 + 15 * diagonal.astype(jnp.int32))
 
     def token(step, device):
@@ -396,6 +406,7 @@
                     gsem["b"].at[0],
                 ).start()
 
+    prepare_right()
     r_turn(1)
     r_turn(3)
     pl.semaphore_wait(tokens.at[0], 7)
@@ -404,6 +415,7 @@
     def _(k):
         token(1, at(p, c, q, lax.rem(z + k, NZ)))
 
+    prepare_weights()
     got(l_all.at[r, q], "a", 0)
     l_up(0).start()
     l_down(0).start()
@@ -413,41 +425,41 @@
     r_step(1, 0)
     pl.semaphore_wait(tokens.at[2], 1)
     own_send()
+    l_step(1)
     own_left()
-    l_step(1)
     r_turn(2)
+    l_sides(0)
     r_step(1, 1)
-    l_sides(0)
+    l_step(2)
     z_step(1, 0)
-    l_step(2)
     r_step(1, 3)
     r_step(1, 2)
-    l_far(0)
-    z_step(2, 0)
     l_sides(1)
     l_step(3)
     own_right()
+    z_step(2, 0)
     r_step(2, 0)
     r_step(2, 1)
-    z_step(3, 0)
-    l_far(1)
+    l_sides(2)
     l_step(4)
     r_step(2, 3)
     z_step(1, 1)
-    l_sides(2)
+    z_step(3, 0)
     r_step(2, 2)
-    z_step(4, 0)
+    l_far(0)
+    l_sides(3)
     r_step(3, 0)
     z_step(2, 1)
-    l_far(2)
-    l_sides(3)
+    z_step(4, 0)
+    l_sides(4)
+    l_far(1)
     r_step(3, 1)
     r_step(3, 3)
+    l_far(2)
+    prepare_own(0, lhs_l)
+    r_step(3, 2)
     z_step(3, 1)
-    l_sides(4)
     l_far(3)
-    r_step(3, 2)
-    prepare_own(0, lhs_l)
     direct(1 - ylo, c)
     l_far(4)
     r_step(4, 0)
@@ -468,9 +480,18 @@
     from_partner(r_all, "rp", 0)
     direct(ylo, 1 - c)
 
-    for i in range(16):
-        both = acc[:, i * 128 : (i + 1) * 128].T
-        middle = pair[i].astype(jnp.float32) + both * (0.5 / 512.0) + bias_ref[...]
+    def out_copy(part):
+        span = pl.ds(part * (16 // PARTS), 16 // PARTS)
+        return pltpu.make_async_copy(
+            out_buf.at[span], out_ref.at[span], gsem["own"].at[9 + part]
+        )
+
+    rows = 16 // PARTS
+    for part in range(PARTS):
+        span = range(part * rows, (part + 1) * rows)
+        both = jnp.concatenate([acc[:, i * 128 : (i + 1) * 128].T for i in span], axis=0)
+        residual = pair[part * rows : (part + 1) * rows].reshape(rows * 128, 128)
+        middle = residual.astype(jnp.float32) + both * (0.5 / 512.0) + bias_ref[...]
         values = middle.astype(jnp.bfloat16).astype(jnp.float32)
         center = jnp.mean(values, axis=1, keepdims=True)
         spread = jnp.mean(jnp.square(values - center), axis=1, keepdims=True)
@@ -480,7 +501,9 @@
         )
         hidden = jnp.maximum(hidden + upb_ref[...], 0.0).astype(jnp.bfloat16)
         result = jnp.dot(hidden, down_w[...], preferred_element_type=jnp.float32)
-        out_ref[i] = (values + result + downb_ref[...]).astype(jnp.bfloat16)
+        result = (values + result + downb_ref[...]).astype(jnp.bfloat16)
+        out_buf[part * rows : (part + 1) * rows] = result.reshape(rows, 128, 128)
+        out_copy(part).start()
 
     @pl.when(diagonal)
     def _():
@@ -496,6 +519,8 @@
     left(r_all.at[pl.ds(0, 15)], "r")
     left(l_all.at[pl.ds(0, 14)], "l")
     left(l_all.at[pl.ds(0, 10), 0], "near")
+    for part in range(PARTS):
+        out_copy(part).wait()
 
 
 def on_device(
@@ -503,15 +528,20 @@
     up_weight, up_bias, down_weight, down_bias,
 ):
     any_spec = pl.BlockSpec(memory_space=pl.ANY)
-    near = pl.BlockSpec(memory_space=pltpu.VMEM)
     bf16, f32 = jnp.bfloat16, jnp.float32
     sems = [pltpu.SemaphoreType.DMA(shape) for shape in ARRIVALS.values()]
     return pl.pallas_call(
         fused_kernel,
         out_shape=jax.ShapeDtypeStruct((16, 128, 128), bf16),
-        in_specs=[any_spec, near] + [any_spec] * 4 + [near] * 4,
-        out_specs=near,
+        in_specs=[any_spec] * 10,
+        out_specs=any_spec,
         scratch_shapes=[
+            pltpu.VMEM((128, 2, 128), bf16),
+            pltpu.VMEM((1, 128), f32),
+            pltpu.VMEM((1, 128), f32),
+            pltpu.VMEM((1, 512), f32),
+            pltpu.VMEM((1, 128), f32),
+            pltpu.VMEM((16, 128, 128), bf16),
             pltpu.VMEM((16, 4, 128, 256), bf16),
             pltpu.VMEM((16, 4, 2, 2, 64, 128), bf16),
             pltpu.VMEM((8, 2, 4, 16, 512), bf16),

time: 68.8 us -> 63.3 us (0.920); the launches traced: 68.6 us -> 62.3 us
  Pallas kernels: 66.7 us -> 60.4 us
    pallas_call x1, Pallas kernels: 66.7 us -> 60.4 us  [on_device(): pl.pallas_call(fused_kernel, out_shape=jax.ShapeDtypeStruct((16, 128, 128...]
where the time goes in v4:
time: 63.3 us; the launch traced here: 62.3 us
  Pallas kernels  60.4 us (95%)
  local copies, waits for them, and re-layouts  1.89 us (3%)
    pallas_call x1, Pallas kernels, on_device(): pl.pallas_call(fused_kernel, out_shape=jax.ShapeDtypeStruct((16, 128, 128...  60.4 us
    unnamed x1, local copies, waits for them, and re-layouts  1.89 us

profile of v4, /device:TPU:1, one launch (start us, length us, event | category | flops | bytes accessed | tf_op | source)
XLA Modules:
  0.0 62.3 jit_solution(5168622701189782170)
XLA Ops:
  0.0 60.4 %gather_and_refine.1 = bf16[16,128,128]{2,1,0:T(8,128)(2,1)} custom-call(bf16[32,64,128]{2,1,0:T(8,128)(2,1)} %bitcast.5, bf16[128,2,128]{2,1,0:T(2,128)(2,1)} %r_src.1, bf16[1024,128]{1,0:T(8,128)(2,1)} %w_src.1, bf16[16,128,128]{2,1,0:T(8,128)(2,1)} %pair_src.1, bf16[128,512]{1,0:T(8,128)(2,1)} %up_src.1, bf16[512,128]{1,0:T(8,128)(2,1)} %down_src.1, ...), custom_call_target="tpu_custom_call" | custom-call | tf_op jit(solution)/shard_map/gather_and_refine/pallas_call | solution.py:533
  60.4 1.9 %copy.12 = bf16[16,128,128]{2,1,0:T(8,128)(2,1)} copy(bf16[16,128,128]{2,1,0:T(8,128)(2,1)} %gather_and_refine.1) | data formatting | bytes 1048576

commit v5 on v4

--- a/solution.py
+++ b/solution.py
@@ -12,7 +12,7 @@
 
 ARRIVALS = {
     "a": (1,), "b": (1,), "c": (1,), "z": (4, 2), "rx": (4,), "r": (4, 4), "rp": (2,),
-    "lx": (5, 2), "l": (4,), "lp": (2,), "own": (13,),
+    "lx": (5, 2), "l": (4,), "lp": (2,), "own": (14,),
 }
 DEPARTURES = ("a", "b", "c", "z", "r", "l", "near")
 LEAVES_BY = {"rp": "r", "lx": "l", "lp": "l", "rx": "near", "l": "near"}
@@ -20,7 +20,7 @@
 
 def fused_kernel(
     l_src, r_src, w_src, pair_src, up_src, down_src, bias_src, gain_src, upb_src,
-    downb_src, out_ref, r_in, bias_ref, gain_ref, upb_ref, downb_ref, out_buf, r_all, l_all, own, r_own, lhs_l, lhs_r, wide, w_in, w_wide, wd,
+    downb_src, out_ref, l_in, r_in, bias_ref, gain_ref, upb_ref, downb_ref, r_all, l_all, own, r_own, lhs_l, lhs_r, wide, w_in, w_wide, wd,
     wm, pair, up_w, down_w, acc, tokens, *sems,
 ):
     gsem = dict(zip(ARRIVALS, sems))
@@ -106,6 +106,8 @@
     ]
     first = pltpu.make_async_copy(r_src, r_in, gsem["own"].at[8])
     first.start()
+    second = pltpu.make_async_copy(l_src, l_in, gsem["own"].at[13])
+    second.start()
 
     greet(partner)
     for k in range(1, NX):
@@ -127,6 +129,7 @@
 
     mine = r_all.at[r, q]
     first.wait()
+    second.wait()
     for e in range(2):
         mine[:, e * 128 : (e + 1) * 128] = r_in[:, e, :]
 
@@ -164,7 +167,7 @@
 
     def a_copy(row):
         return send(
-            l_src.at[pl.ds(2 * row, 2)], l_all.at[row, q, c], "a", 0,
+            l_in.at[pl.ds(2 * row, 2)], l_all.at[row, q, c], "a", 0,
             {"row": row, "col": z, "seq": q},
         )
 
@@ -176,7 +179,7 @@
         )
 
     def c_source(qq):
-        return l_src.at[pl.ds(4 * z, 4), pl.ds(pl.multiple_of(qq * 16, 16), 16)]
+        return l_in.at[pl.ds(4 * z, 4), pl.ds(pl.multiple_of(qq * 16, 16), 16)]
 
     def c_copy(k):
         qq = lax.rem(q + k, 4)
@@ -249,7 +252,7 @@
     @pl.when(diagonal)
     def _():
         pltpu.make_async_copy(
-            l_src.at[pl.ds(2 * r, 2)], l_all.at[r, q, c], gsem["a"].at[0]
+            l_in.at[pl.ds(2 * r, 2)], l_all.at[r, q, c], gsem["a"].at[0]
         ).start()
 
         @pl.loop(1, 16)
@@ -431,34 +434,34 @@
     l_sides(0)
     r_step(1, 1)
     l_step(2)
-    z_step(1, 0)
+    own_right()
     r_step(1, 3)
     r_step(1, 2)
-    l_sides(1)
+    z_step(1, 0)
     l_step(3)
-    own_right()
-    z_step(2, 0)
     r_step(2, 0)
     r_step(2, 1)
-    l_sides(2)
+    l_sides(1)
+    z_step(1, 1)
+    z_step(2, 0)
     l_step(4)
     r_step(2, 3)
-    z_step(1, 1)
+    r_step(2, 2)
+    l_sides(2)
+    z_step(2, 1)
     z_step(3, 0)
-    r_step(2, 2)
     l_far(0)
+    r_step(3, 0)
     l_sides(3)
-    r_step(3, 0)
-    z_step(2, 1)
+    z_step(3, 1)
     z_step(4, 0)
-    l_sides(4)
-    l_far(1)
     r_step(3, 1)
     r_step(3, 3)
-    l_far(2)
+    l_far(1)
+    l_sides(4)
     prepare_own(0, lhs_l)
     r_step(3, 2)
-    z_step(3, 1)
+    l_far(2)
     l_far(3)
     direct(1 - ylo, c)
     l_far(4)
@@ -480,12 +483,6 @@
     from_partner(r_all, "rp", 0)
     direct(ylo, 1 - c)
 
-    def out_copy(part):
-        span = pl.ds(part * (16 // PARTS), 16 // PARTS)
-        return pltpu.make_async_copy(
-            out_buf.at[span], out_ref.at[span], gsem["own"].at[9 + part]
-        )
-
     rows = 16 // PARTS
     for part in range(PARTS):
         span = range(part * rows, (part + 1) * rows)
@@ -502,8 +499,7 @@
         hidden = jnp.maximum(hidden + upb_ref[...], 0.0).astype(jnp.bfloat16)
         result = jnp.dot(hidden, down_w[...], preferred_element_type=jnp.float32)
         result = (values + result + downb_ref[...]).astype(jnp.bfloat16)
-        out_buf[part * rows : (part + 1) * rows] = result.reshape(rows, 128, 128)
-        out_copy(part).start()
+        out_ref[part * rows : (part + 1) * rows] = result.reshape(rows, 128, 128)
 
     @pl.when(diagonal)
     def _():
@@ -519,29 +515,26 @@
     left(r_all.at[pl.ds(0, 15)], "r")
     left(l_all.at[pl.ds(0, 14)], "l")
     left(l_all.at[pl.ds(0, 10), 0], "near")
-    for part in range(PARTS):
-        out_copy(part).wait()
 
 
 def on_device(
     left_piece, right_piece, proj_weight, proj_bias, pair_rep, norm_gain,
     up_weight, up_bias, down_weight, down_bias,
 ):
-    any_spec = pl.BlockSpec(memory_space=pl.ANY)
     bf16, f32 = jnp.bfloat16, jnp.float32
     sems = [pltpu.SemaphoreType.DMA(shape) for shape in ARRIVALS.values()]
     return pl.pallas_call(
         fused_kernel,
         out_shape=jax.ShapeDtypeStruct((16, 128, 128), bf16),
-        in_specs=[any_spec] * 10,
-        out_specs=any_spec,
+        in_specs=[pl.BlockSpec(memory_space=pltpu.HBM)] * 10,
+        out_specs=pl.BlockSpec(memory_space=pltpu.VMEM),
         scratch_shapes=[
+            pltpu.VMEM((32, 64, 128), bf16),
             pltpu.VMEM((128, 2, 128), bf16),
             pltpu.VMEM((1, 128), f32),
             pltpu.VMEM((1, 128), f32),
             pltpu.VMEM((1, 512), f32),
             pltpu.VMEM((1, 128), f32),
-            pltpu.VMEM((16, 128, 128), bf16),
             pltpu.VMEM((16, 4, 128, 256), bf16),
             pltpu.VMEM((16, 4, 2, 2, 64, 128), bf16),
             pltpu.VMEM((8, 2, 4, 16, 512), bf16),
@@ -562,13 +555,17 @@
         + sems
         + [pltpu.SemaphoreType.DMA((len(DEPARTURES),))],
         compiler_params=pltpu.CompilerParams(
-            collective_id=0, has_side_effects=True, vmem_limit_bytes=56 << 20
+            collective_id=0, has_side_effects=True, vmem_limit_bytes=32 << 20
         ),
         name="gather_and_refine",
     )(
-        left_piece.transpose(1, 2, 0), right_piece, proj_weight, pair_rep, up_weight,
+        *(
+            pltpu.with_memory_space_constraint(array, pltpu.HBM)
+            for array in (        left_piece.transpose(1, 2, 0), right_piece, proj_weight, pair_rep, up_weight,
         down_weight, proj_bias.reshape(1, 128), norm_gain.reshape(1, 128),
         up_bias.reshape(1, 512), down_bias.reshape(1, 128),
+            )
+        )
     )
 
 

time: 63.3 us -> 61.7 us (0.975); the launches traced: 62.3 us -> 61.6 us
  local copies, waits for them, and re-layouts: 1.89 us -> 0.8 us
    unnamed x1, local copies, waits for them, and re-layouts: 1.89 us -> 0.8 us
where the time goes in v5:
time: 61.7 us; the launch traced here: 61.6 us
  Pallas kernels  60.7 us (98%)
  local copies, waits for them, and re-layouts  0.8 us (1%)
    pallas_call x1, Pallas kernels, on_device(): pl.pallas_call(fused_kernel, out_shape=jax.ShapeDtypeStruct((16, 128, 128...  60.7 us

profile of v5, /device:TPU:1, one launch (start us, length us, event | category | flops | bytes accessed | tf_op | source)
XLA Modules:
  0.0 61.6 jit_solution(16865219474422100748)
XLA Ops:
  0.0 60.7 %gather_and_refine.1 = bf16[16,128,128]{2,1,0:T(8,128)(2,1)S(1)} custom-call(bf16[32,64,128]{2,1,0:T(8,128)(2,1)} %bitcast.5, bf16[128,2,128]{2,1,0:T(2,128)(2,1)} %r_src.1, bf16[1024,128]{1,0:T(8,128)(2,1)} %w_src.1, bf16[16,128,128]{2,1,0:T(8,128)(2,1)} %pair_src.1, bf16[128,512]{1,0:T(8,128)(2,1)} %up_src.1, bf16[512,128]{1,0:T(8,128)(2,1)} %down_src.1, ...), custom_call_target="tpu_custom_call" | custom-call | tf_op jit(solution)/shard_map/gather_and_refine/pallas_call | solution.py:526
  60.8 0.8 %copy.12 = bf16[16,128,128]{2,1,0:T(8,128)(2,1)} copy(bf16[16,128,128]{2,1,0:T(8,128)(2,1)S(1)} %gather_and_refine.1) | data formatting | bytes 1048576
